TPU v7x, 128 devices: a whole 4x4x4 slice. The times are simulated.
128 devices in a mesh: ty: 8 (over y, core), tx: 16 (over z, x).
Axes of the slice: x: 4, y: 4, z: 4, core: 2. Of those that a mesh axis runs over, the one named last changes fastest.
Arguments:
- covariates: bfloat16 [262144, 512], P(('ty', 'tx')), may hold values from -24 to 24
- w_in: bfloat16 [512, 2048], replicated, may hold values from -0.25 to 0.25
- b_in: float32 [2048], replicated, may hold values from -3 to 3
- w_out: bfloat16 [2048, 128], replicated, may hold values from -0.125 to 0.125
- b_out: float32 [128], replicated, may hold values from -2 to 2
- owner: int32 [262144, 1], P(('ty', 'tx')), may hold values from 0 to 127; in each aligned block of 2048 rows (0 to 2047, 2048 to 4095, ...) at most 32 rows name the same one
- land_cell: int32 [262144], P(('ty', 'tx')), may hold values from 0 to 2047
- row_taps: float32 [128, 9], replicated, may hold values from 0.2 to 1
- col_taps: float32 [128, 9], replicated, may hold values from 0.2 to 1
- rate: float32 [128], replicated, may hold values from 0.2 to 1.5
- capacity: float32 [128], replicated, may hold values from 0.5 to 4
- observed: int32 [128, 2048, 128], P('ty', 'tx'), may hold values from 0 to 2
- surveyed: int32 [128, 2048], P('ty', 'tx'), may hold values 0 or 1
Outputs:
- density: float32 [128, 2048, 128], P('ty', 'tx')
- grad_w_in: float32 [512, 2048], P(('ty', 'tx'))
- grad_w_out: float32 [2048, 128], P(('ty', 'tx'))
Inputs may be any that keep to these rules, and one draw needn't show every extreme that they name: `owner`: among the land cells of one device, no tile owns more than 32, and some tile owns exactly 32.
All inputs are finite; a program needn't handle non-finite values. No bound on the sum of `surveyed` on one device may be relied on, other than what follows from the above.
Results may differ from a plain program's by a relative error of at most 0.0017.
Values may be sent and summed in bfloat16 or wider, within the bound.
No kernel may reach another device: no remote copies, remote signals or barrier semaphores. Data moves between devices by JAX's collectives and lax.ppermute only.
A program may use at most 128 MiB of HBM per device.

v0:
```python
import functools
import math

import jax
import jax.numpy as jnp
from jax import lax
from jax.experimental import pallas as pl
from jax.experimental.pallas import tpu as pltpu
from jax.sharding import Mesh
from jax.sharding import PartitionSpec as P

STEPS = 4
REACH = 4
CHUNK = 64
TY = ("y", "core")
TX = ("z", "x")
ALL = TY + TX
F32 = jnp.float32
BF16 = jnp.bfloat16


def normalize(taps):
    return taps / jnp.sum(taps, axis=1, keepdims=True)


def raster_body(scale, species_ref, got_ref, density_ref, grad_ref, cells, mids, codes):
    rows, across, lanes = codes.shape
    tall = grad_ref.shape[1]
    taps_y = [species_ref[0, k] for k in range(9)]
    taps_x = [species_ref[0, 9 + k] for k in range(9)]
    rate, capacity = species_ref[0, 18], species_ref[0, 19]
    for slot in range(2):
        cells[slot, 0:REACH] = jnp.zeros((REACH, across, lanes), F32)
        cells[slot, REACH + rows :] = jnp.zeros((REACH, across, lanes), F32)
    for band in range(rows // tall):
        at = band * tall
        tiles = slice(band * across, (band + 1) * across)
        start = jnp.swapaxes(got_ref[tiles, 0:tall, :].astype(F32), 0, 1)
        cells[0, REACH + at : REACH + at + tall] = 0.1 + start
        codes[at : at + tall] = jnp.swapaxes(got_ref[tiles, tall : 2 * tall, :].astype(F32), 0, 1)
    block = (CHUNK, across, lanes)
    lane = lax.broadcasted_iota(jnp.int32, block, 2)
    tile = lax.broadcasted_iota(jnp.int32, block, 1)
    from_right = (lane < REACH) & (tile < across - 1)
    from_left = (lane >= lanes - REACH) & (tile > 0)

    def spread(along_x):
        came = lax.broadcasted_iota(jnp.int32, (2 * lanes, lanes), 0)
        goes = lax.broadcasted_iota(jnp.int32, (2 * lanes, lanes), 1)
        beside = jnp.where(came < lanes + lanes // 2, came, came - 2 * lanes)
        tap = jnp.where(came < lanes, came, beside) - goes + REACH
        matrix = jnp.zeros((2 * lanes, lanes), F32)
        for k in range(9):
            matrix = jnp.where(tap == k, along_x[k], matrix)
        high = matrix.astype(BF16)
        return high, (matrix - high.astype(F32)).astype(BF16)

    def disperse(slot, at, along_y, along_x):
        total = None
        for k in range(9):
            part = along_y[k] * cells[slot, pl.ds(at + k, CHUNK)]
            total = part if total is None else total + part
        right = pltpu.roll(total, across - 1, axis=1)
        left = pltpu.roll(total, 1, axis=1)
        edge = jnp.where(from_right, right, jnp.where(from_left, left, 0.0))
        both = jnp.concatenate([total, edge], axis=2).reshape(CHUNK * across, 2 * lanes)
        high = both.astype(BF16)
        low = (both - high.astype(F32)).astype(BF16)
        result = jnp.dot(high, along_x[0], preferred_element_type=F32)
        result = result + jnp.dot(low, along_x[0], preferred_element_type=F32)
        result = result + jnp.dot(high, along_x[1], preferred_element_type=F32)
        return result.reshape(block)

    forth, back = spread(taps_x), spread(taps_x[::-1])

    def each_chunk(do):
        def step(chunk, carry):
            do(chunk * CHUNK)
            return carry

        lax.fori_loop(0, rows // CHUNK, step, 0)

    def forward_step(step, carry):
        slot = step % 2

        def do(at):
            mid = disperse(slot, at, taps_y, forth)
            mids[step, pl.ds(at, CHUNK)] = mid
            field = mid * (1.0 + rate) / (1.0 + mid * (rate / capacity))
            cells[1 - slot, pl.ds(REACH + at, CHUNK)] = field

        each_chunk(do)
        return carry

    lax.fori_loop(0, STEPS, forward_step, 0)
    last = STEPS % 2

    def grown(grad, step, at):
        denom = 1.0 + mids[step, pl.ds(at, CHUNK)] * (rate / capacity)
        return grad * (1.0 + rate) / (denom * denom)

    def loss(at):
        field = cells[last, pl.ds(REACH + at, CHUNK)]
        code = codes[pl.ds(at, CHUNK)]
        grad = jnp.where(code >= 0.0, (1.0 - code / field) * scale, 0.0)
        cells[1 - last, pl.ds(REACH + at, CHUNK)] = grown(grad, STEPS - 1, at)

    each_chunk(loss)
    for band in range(rows // tall):
        at = band * tall
        density_ref[band * across : (band + 1) * across] = jnp.swapaxes(
            cells[last, REACH + at : REACH + at + tall], 0, 1
        )

    def backward_step(step, carry):
        slot = (1 - last + step) % 2

        def do(at):
            grad = disperse(slot, at, taps_y[::-1], back)
            cells[1 - slot, pl.ds(REACH + at, CHUNK)] = grown(grad, STEPS - 2 - step, at)

        each_chunk(do)
        return carry

    lax.fori_loop(0, STEPS - 1, backward_step, 0)
    slot = (1 - last + STEPS - 1) % 2

    def final(at):
        codes[pl.ds(at, CHUNK)] = disperse(slot, at, taps_y[::-1], back)

    each_chunk(final)
    for band in range(rows // tall):
        at = band * tall
        grad_ref[band * across : (band + 1) * across] = jnp.swapaxes(
            codes[at : at + tall], 0, 1
        ).astype(BF16)


def raster(species, got, scale, tiles_y, tiles_x):
    tiles, two, lanes = got.shape
    tall = two // 2
    rows = tiles_y * tall

    def whole(shape):
        return pl.BlockSpec(shape, lambda: (0,) * len(shape))

    return pl.pallas_call(
        functools.partial(raster_body, scale),
        out_shape=[
            jax.ShapeDtypeStruct((tiles, tall, lanes), F32),
            jax.ShapeDtypeStruct((tiles, tall, lanes), BF16),
        ],
        in_specs=[pl.BlockSpec(memory_space=pltpu.SMEM), whole(got.shape)],
        out_specs=[whole((tiles, tall, lanes))] * 2,
        scratch_shapes=[
            pltpu.VMEM((2, rows + 2 * REACH, tiles_x, lanes), F32),
            pltpu.VMEM((STEPS, rows, tiles_x, lanes), F32),
            pltpu.VMEM((rows, tiles_x, lanes), F32),
        ],
        compiler_params=pltpu.CompilerParams(vmem_limit_bytes=48 << 20),
        name="raster_steps",
    )(species, got)


def forward_body(x_ref, w_in_ref, b_in_ref, w_out_ref, b_out_ref, intensity_ref):
    chunk = 512
    x = x_ref[...]
    log_rate = b_out_ref[...]
    for at in range(0, w_in_ref.shape[1], chunk):
        pre = jnp.dot(x, w_in_ref[:, at : at + chunk], preferred_element_type=F32)
        pre = pre + b_in_ref[:, at : at + chunk]
        hidden = (pre / (1.0 + jnp.exp(-pre))).astype(BF16)
        log_rate = log_rate + jnp.dot(
            hidden, w_out_ref[at : at + chunk, :], preferred_element_type=F32
        )
    intensity_ref[...] = jnp.exp(log_rate)


def forward(x, w_in, b_in, w_out, b_out, block=512):
    rows, cov = x.shape
    hid, species = w_out.shape

    def whole(shape):
        return pl.BlockSpec(shape, lambda i: (0, 0), pipeline_mode=pl.Buffered(1))

    return pl.pallas_call(
        forward_body,
        out_shape=jax.ShapeDtypeStruct((rows, species), F32),
        grid=(rows // block,),
        in_specs=[
            pl.BlockSpec((block, cov), lambda i: (i, 0)),
            whole((cov, hid)),
            whole((1, hid)),
            whole((hid, species)),
            whole((1, species)),
        ],
        out_specs=pl.BlockSpec((block, species), lambda i: (i, 0)),
        compiler_params=pltpu.CompilerParams(vmem_limit_bytes=40 << 20),
        name="land_forward",
    )(x, w_in, b_in[None, :], w_out, b_out[None, :])


def gates_body(core_ref, x_ref, w_in_ref, b_in_ref, hidden_ref, slope_ref):
    pre = jnp.dot(x_ref[...], w_in_ref[...], preferred_element_type=F32) + b_in_ref[...]
    gate = 1.0 / (1.0 + jnp.exp(-pre))
    scaled = pre * gate
    hidden_ref[...] = scaled.astype(BF16)
    slope_ref[...] = gate + scaled * (1.0 - gate)


def gates(core, x, w_in, b_in):
    n_y = 4
    rows, cov = x.shape
    hid = w_in.shape[1]
    width = hid // n_y // 2
    block = pl.BlockSpec((rows, width), lambda j, c: (0, j))
    return pl.pallas_call(
        gates_body,
        out_shape=[
            jax.ShapeDtypeStruct((rows, hid // 2), BF16),
            jax.ShapeDtypeStruct((rows, hid // 2), F32),
        ],
        grid_spec=pltpu.PrefetchScalarGridSpec(
            num_scalar_prefetch=1,
            grid=(n_y,),
            in_specs=[
                pl.BlockSpec((rows, cov), lambda j, c: (0, 0), pipeline_mode=pl.Buffered(1)),
                pl.BlockSpec((cov, width), lambda j, c: (0, 2 * j + c[0])),
                pl.BlockSpec((1, width), lambda j, c: (0, 2 * j + c[0])),
            ],
            out_specs=[block, block],
        ),
        compiler_params=pltpu.CompilerParams(vmem_limit_bytes=40 << 20),
        name="land_gates",
    )(core, x, w_in, b_in[None, :])


def backward_body(
    core_ref,
    x_own,
    x_other,
    dlog_own,
    dlog_other,
    hidden_own,
    hidden_other,
    slope_own,
    slope_other,
    w_out_ref,
    out_ref,
    in_acc,
    out_acc,
):
    j = pl.program_id(0)
    w_out = w_out_ref[...]

    def parts(x_ref, dlog_ref, hidden_ref, slope_ref):
        dlog = dlog_ref[...]
        dhidden = lax.dot_general(
            dlog, w_out, (((1,), (1,)), ((), ())), preferred_element_type=F32
        )
        dpre = (dhidden * slope_ref[...]).astype(BF16)
        rows = (((0,), (0,)), ((), ()))
        return (
            lax.dot_general(x_ref[...], dpre, rows, preferred_element_type=F32),
            lax.dot_general(hidden_ref[...], dlog, rows, preferred_element_type=F32),
        )

    in_acc[...], out_acc[...] = parts(x_own, dlog_own, hidden_own, slope_own)
    in_part, out_part = parts(x_other, dlog_other, hidden_other, slope_other)
    in_acc[...] += in_part
    out_acc[...] += out_part
    n_y = 4
    zx = out_ref.shape[0] // n_y
    tiles = in_acc.shape[1] // 128
    rows = in_acc.shape[0] // out_ref.shape[0] // 2
    units = out_acc.shape[0] // zx
    for y in range(n_y):
        for p in range(zx):
            for c in range(2):
                for k in range(tiles):
                    out_ref[
                        y * zx + p, pl.ds((j * tiles + k) * 2 * rows + c * rows, rows), :
                    ] = in_acc[
                        pl.ds((y * 2 * zx + c * zx + p) * rows, rows),
                        k * 128 : (k + 1) * 128,
                    ]
    base = 2 * rows * tiles * n_y
    for p in range(zx):
        out_ref[j * zx + p, base : base + units, :] = out_acc[p * units : (p + 1) * units, :]


def backward(core, x, dlog, hidden, slope, w_out, peers):
    n_y = 4
    rows, cov = x[0].shape
    hid, species = w_out.shape
    width = hid // n_y // 2
    send_rows = cov // peers * (hid // 2 // 128) + hid // 2 // peers

    def fixed(shape):
        return pl.BlockSpec(
            shape, lambda j, c: (0,) * len(shape), pipeline_mode=pl.Buffered(1)
        )

    grid_spec = pltpu.PrefetchScalarGridSpec(
        num_scalar_prefetch=1,
        grid=(n_y,),
        in_specs=[fixed((rows, cov))] * 2
        + [fixed((rows, species))] * 2
        + [pl.BlockSpec((rows, width), lambda j, c: (0, j))] * 4
        + [pl.BlockSpec((width, species), lambda j, c: (2 * j + c[0], 0))],
        out_specs=fixed((peers, send_rows, 128)),
        scratch_shapes=[pltpu.VMEM((cov, width), F32), pltpu.VMEM((width, species), F32)],
    )
    return pl.pallas_call(
        backward_body,
        out_shape=jax.ShapeDtypeStruct((peers, send_rows, 128), F32),
        grid_spec=grid_spec,
        compiler_params=pltpu.CompilerParams(vmem_limit_bytes=50 << 20),
        name="land_backward",
    )(core, *x, *dlog, *hidden, *slope, w_out)


def pick_body(wide, index_ref, table_ref, *refs):
    index = index_ref[...]
    out_ref = refs[-1]
    lanes = out_ref.shape[1]
    if wide:
        keys = table_ref.shape[1] // 2
        table = jnp.concatenate([table_ref[:, :keys], table_ref[:, keys:]], axis=0)
        dims = (((1,), (1,)), ((), ()))
    else:
        keys = table_ref.shape[0] // 2
        table = jnp.concatenate([table_ref[:keys, :], table_ref[keys:, :]], axis=1)
        dims = (((1,), (0,)), ((), ()))
    upper = index >= keys
    key = jnp.where(upper, index - keys, index)
    ids = lax.broadcasted_iota(jnp.int32, (index.shape[0], keys), 1)
    hot = jnp.where(ids == key, 1.0, 0.0).astype(BF16)
    both = lax.dot_general(hot, table, dims, preferred_element_type=F32)
    picked = jnp.where(upper, both[:, lanes:], both[:, :lanes])
    if len(refs) > 1:
        picked = picked * refs[0][...]
    out_ref[...] = picked.astype(BF16)


def pick(index, table, factors=None, wide=False, block=512):
    rows = index.shape[0]
    lanes = table.shape[0] if wide else table.shape[1]
    block_spec = pl.BlockSpec((block, lanes), lambda i: (i, 0))
    more = () if factors is None else (factors,)
    return pl.pallas_call(
        functools.partial(pick_body, wide),
        out_shape=jax.ShapeDtypeStruct((rows, lanes), BF16),
        grid=(rows // block,),
        in_specs=[
            pl.BlockSpec((block, 1), lambda i: (i, 0)),
            pl.BlockSpec(table.shape, lambda i: (0, 0), pipeline_mode=pl.Buffered(1)),
        ]
        + [block_spec] * len(more),
        out_specs=block_spec,
        compiler_params=pltpu.CompilerParams(vmem_limit_bytes=40 << 20),
        name="pick_rows",
    )(index[:, None], table, *more)


def other_core(values):
    return lax.ppermute(values, "core", [(0, 1), (1, 0)])


def local(
    covariates,
    w_in,
    b_in,
    w_out,
    b_out,
    owner,
    land_cell,
    row_taps,
    col_taps,
    rate,
    capacity,
    observed,
    surveyed,
):
    row_count = covariates.shape[0]
    tiles_y = lax.axis_size("y") * lax.axis_size("core")
    tiles_x = lax.axis_size("z") * lax.axis_size("x")
    devices = tiles_y * tiles_x
    slot_count = 2 * row_count // devices
    slots = devices * slot_count
    height, tile_width, species = observed.shape
    cell_count = height * tile_width
    core = lax.axis_index("core")
    theirs = other_core(covariates)
    intensity = forward(covariates, w_in, b_in, w_out, b_out)

    owner_rows = owner[:, 0]
    owner_hot = owner_rows[:, None] == jnp.arange(devices, dtype=jnp.int32)[None, :]
    row_ids = jnp.arange(row_count, dtype=jnp.int32)
    earlier = (row_ids[None, :] < row_ids[:, None]).astype(BF16)
    before = jnp.dot(earlier, owner_hot.astype(BF16), preferred_element_type=F32)
    slot_idx = jnp.sum(jnp.where(owner_hot, before, 0.0), axis=1).astype(jnp.int32)
    flat_slot = owner_rows * slot_count + slot_idx

    upper = flat_slot >= slots // 2
    slot_ids = jnp.arange(slots // 2, dtype=jnp.int32)
    slot_key = jnp.where(upper, flat_slot - slots // 2, flat_slot)
    pack = (slot_key[None, :] == slot_ids[:, None]).astype(BF16)
    halves = jnp.concatenate(
        [jnp.where(upper[:, None], 0.0, intensity), jnp.where(upper[:, None], intensity, 0.0)],
        axis=1,
    ).astype(BF16)
    packed = jnp.dot(pack, halves, preferred_element_type=F32).astype(BF16)
    send_values = jnp.concatenate([packed[:, :species], packed[:, species:]])
    slot_hot = jnp.arange(slot_count, dtype=jnp.int32)[:, None] == slot_idx[None, :]
    place_row = (land_cell // tile_width + 1).astype(F32)[None, :]
    place_col = (land_cell % tile_width).astype(F32)[None, :]
    places = jnp.concatenate(
        [jnp.where(slot_hot, place_row, 0.0), jnp.where(slot_hot, place_col, 0.0)], axis=0
    ).astype(BF16)
    table = jnp.dot(places, owner_hot.astype(BF16), preferred_element_type=F32).astype(BF16).T
    table = jnp.pad(table[:, None, :], ((0, 0), (0, 7), (0, species - 2 * slot_count)))
    send = jnp.concatenate([send_values.reshape(devices, slot_count, species), table], axis=1)
    got = lax.all_to_all(send, ALL, split_axis=0, concat_axis=0, tiled=True)
    send, own = lax.optimization_barrier((send, covariates))
    own_gates = gates(core[None], own, w_in, b_in)
    got, own_gates = lax.optimization_barrier((got, own_gates))
    got_values = got[:, :slot_count].reshape(slots, species)
    got_row = got[:, slot_count, :slot_count].astype(jnp.int32)
    got_col = got[:, slot_count, slot_count : 2 * slot_count].astype(jnp.int32)
    cell_list = jnp.where(got_row > 0, (got_row - 1) * tile_width + got_col, -1).reshape(-1)
    cell_ids = jnp.arange(cell_count, dtype=jnp.int32)
    place = (cell_list[None, :] == cell_ids[:, None]).astype(BF16)
    start_field = jnp.dot(place, got_values, preferred_element_type=F32)

    code = jnp.where(surveyed[:, :, None] > 0, observed, -1).astype(BF16)
    send = jnp.concatenate(
        [
            start_field.astype(BF16).T.reshape(species, height, tile_width),
            code.reshape(cell_count, species).T.reshape(species, height, tile_width),
        ],
        axis=1,
    )
    traits = jnp.concatenate(
        [normalize(row_taps), normalize(col_taps), rate[:, None], capacity[:, None]], axis=1
    )
    traits = jnp.pad(traits, ((0, 0), (0, 32 - traits.shape[1])))
    traits = lax.dynamic_slice_in_dim(traits, lax.axis_index(ALL), 1, axis=0)
    scale = 1.0 / math.sqrt(row_count * devices)
    got = lax.all_to_all(send, ALL, 0, 0, tiled=True)
    send, theirs = lax.optimization_barrier((send, theirs))
    their_gates = gates(core[None], theirs, w_in, b_in)
    got, their_gates = lax.optimization_barrier((got, their_gates))
    density, grad_start = raster(traits, got, scale, tiles_y, tiles_x)
    grad_start = lax.all_to_all(grad_start, ALL, 0, 0, tiled=True).reshape(species, cell_count)

    back_values = pick(cell_list, grad_start, wide=True)
    home_values = lax.all_to_all(
        back_values.reshape(devices, slot_count, species),
        ALL,
        split_axis=0,
        concat_axis=0,
        tiled=True,
    )
    home_values, density = lax.optimization_barrier((home_values, density))
    density = lax.all_to_all(density, ALL, 0, 0, tiled=True)
    dlog = pick(flat_slot, home_values.reshape(slots, species), intensity)
    peers = devices // 2
    pieces = backward(
        core[None],
        (covariates, theirs),
        (dlog, other_core(dlog)),
        (own_gates[0], their_gates[0]),
        (own_gates[1], their_gates[1]),
        w_out,
        peers,
    )
    pieces, density = lax.optimization_barrier((pieces, density))
    density = density.reshape(species, cell_count).T.reshape(height, tile_width, species)
    pieces = lax.all_to_all(pieces, ("y", "z", "x"), 0, 0)
    pieces, density = lax.optimization_barrier((pieces, density))
    pieces = jnp.sum(pieces, axis=0)
    hid, cov = w_in.shape[1], w_in.shape[0]
    rows_in = cov // devices
    in_rows = 2 * rows_in * (hid // 2 // species)
    grad_w_out = pieces[in_rows:]
    halves = pieces[:in_rows].reshape(4, hid // 8 // species, 2, rows_in, species)
    mine = lax.dynamic_index_in_dim(halves, core, 2, keepdims=False)
    sent_over = other_core(lax.dynamic_index_in_dim(halves, 1 - core, 2, keepdims=False))
    first, second = jnp.where(core == 0, mine, sent_over), jnp.where(core == 0, sent_over, mine)
    grad_w_in = jnp.stack([first, second], axis=1)
    grad_w_in = grad_w_in.transpose(3, 0, 1, 2, 4).reshape(rows_in, hid)
    return (density, grad_w_in, grad_w_out)


def solution(mesh):
    tiles_y, tiles_x = mesh.devices.shape
    split = Mesh(mesh.devices.reshape(tiles_y // 2, 2, tiles_x // 4, 4), ALL)
    in_specs = (
        P(ALL, None),
        P(),
        P(),
        P(),
        P(),
        P(ALL, None),
        P(ALL),
        P(),
        P(),
        P(),
        P(),
        P(TY, TX, None),
        P(TY, TX),
    )
    out_specs = (P(TY, TX, None), P(ALL, None), P(ALL, None))
    return jax.shard_map(local, mesh=split, in_specs=in_specs, out_specs=out_specs, check_vma=False)
```

profile of v0, /device:TPU:0, one launch (start us, length us, event | category | flops | bytes accessed | tf_op | source)
XLA Modules:
  0.0 241.6 jit_solution(5253444349533263347)
XLA Ops:
  0.7 3.4 %fusion.11 = f32[2048]{0:T(1024)S(1)} fusion(s32[2048]{0:T(1024)} %bitcast.73), kind=kOutput, calls=%fused_computation.15 | convolution fusion | flops 1078982656 | bytes 16384 | tf_op jit(solution)/shard_map/dot_general | solution.py:401
  4.2 8.9 %land_forward.1.refs_0_ = f32[2048,128]{1,0:T(8,128)S(1)} custom-call(bf16[2048,512]{1,0:T(8,128)(2,1)S(1)} %copy-done, bf16[512,2048]{1,0:T(8,128)(2,1)S(1)} %copy-done.1, f32[1,2048]{1,0:T(1,128)S(1)} %bitcast.57, bf16[2048,128]{1,0:T(8,128)(2,1)S(1)} %copy-done.9, f32[1,128]{1,0:T(1,128)S(1)} %bitcast.60), custom_call_target="tpu_custom_call" | custom-call | tf_op jit(solution)/shard_map/land_forward/pallas_call | solution.py:186
  13.6 3.2 %fusion.6 = bf16[2048,256]{1,0:T(8,128)(2,1)S(1)} fusion(s32[2048]{0:T(1024)S(1)} %compare_select_fusion.1, bf16[2048,128]{1,0:T(8,128)(2,1)S(1)} %get-tuple-element.48, bf16[2048,128]{1,0:T(8,128)(2,1)S(1)} %get-tuple-element.47), kind=kOutput, calls=%fused_computation.10 | convolution fusion | flops 2154299392 | bytes 2105344 | tf_op jit(solution)/shard_map/dot_general | solution.py:413
  21.1 11.6 %all-to-all-start = ((bf16[128,40,128]{2,1,0:T(8,128)(2,1)}), bf16[128,40,128]{2,1,0:T(8,128)(2,1)}, u32[]{:S(2)}, u32[]{:S(2)}) async-start(bf16[128,40,128]{2,1,0:T(8,128)(2,1)} %fusion.9), calls=%async_computation | async-start | bytes 2621440 | tf_op jit(solution)/shard_map/all_to_all | solution.py:424
  33.0 2.4 select_convert_fusion
  41.0 6.3 %land_gates.2 = (bf16[2048,1024]{1,0:T(8,128)(2,1)S(1)}, f32[2048,1024]{1,0:T(8,128)}) custom-call(s32[1]{0:T(128)} %bitcast.core_ref, bf16[2048,512]{1,0:T(8,128)(2,1)S(1)} %copy-done, bf16[512,2048]{1,0:T(8,128)(2,1)S(1)} %copy-done.2, f32[1,2048]{1,0:T(1,128)S(1)} %bitcast.58), custom_call_target="tpu_custom_call" | custom-call | tf_op jit(solution)/shard_map/land_gates/pallas_call | solution.py:217
  49.2 4.9 %all-to-all-done = bf16[128,40,128]{2,1,0:T(8,128)(2,1)} async-done(((bf16[128,40,128]{2,1,0:T(8,128)(2,1)}), bf16[128,40,128]{2,1,0:T(8,128)(2,1)}, u32[]{:S(2)}, u32[]{:S(2)}) %all-to-all-start) | async-done | bytes 1310752 | tf_op jit(solution)/shard_map/all_to_all | solution.py:424
  59.1 8.5 %fusion.10 = bf16[16,8,16,128]{3,1,2,0:T(8,128)(2,1)S(1)} fusion(bf16[4096,128]{1,0:T(8,128)(2,1)} %bitcast.68, s32[4096]{0:T(1024)S(1)} %reshape.152), kind=kOutput, calls=%fused_computation.14 | convolution fusion | flops 2156134400 | bytes 1589248 | tf_op jit(solution)/shard_map/dot_general | solution.py:434
  69.6 6.0 %all-to-all-start.1 = ((bf16[128,32,128]{2,1,0:T(8,128)(2,1)}), bf16[128,32,128]{2,1,0:T(8,128)(2,1)}, u32[]{:S(2)}, u32[]{:S(2)}) async-start(bf16[128,32,128]{2,1,0:T(8,128)(2,1)} %constant_dynamic-update-slice_fusion), calls=%async_computation.1 | async-start | bytes 2097152 | tf_op jit(solution)/shard_map/all_to_all | solution.py:450
  77.4 7.8 %land_gates.3 = (bf16[2048,1024]{1,0:T(8,128)(2,1)S(1)}, f32[2048,1024]{1,0:T(8,128)}) custom-call(s32[1]{0:T(128)} %bitcast.core_ref, bf16[2048,512]{1,0:T(8,128)(2,1)} %collective-permute-done.x_ref.x_other, bf16[512,2048]{1,0:T(8,128)(2,1)S(1)} %copy-done.3, f32[1,2048]{1,0:T(1,128)S(1)} %bitcast.59), custom_call_target="tpu_custom_call" | custom-call | tf_op jit(solution)/shard_map/land_gates/pallas_call | solution.py:217
  87.2 6.7 %all-to-all-done.1.got_ref = bf16[128,32,128]{2,1,0:T(8,128)(2,1)} async-done(((bf16[128,32,128]{2,1,0:T(8,128)(2,1)}), bf16[128,32,128]{2,1,0:T(8,128)(2,1)}, u32[]{:S(2)}, u32[]{:S(2)}) %all-to-all-start.1) | async-done | bytes 1048608 | tf_op jit(solution)/shard_map/all_to_all | solution.py:450
  93.9 15.4 %raster_steps.1 = (f32[128,16,128]{2,1,0:T(8,128)S(1)}, bf16[128,16,128]{2,1,0:T(8,128)(2,1)S(1)}) custom-call(f32[1,32]{1,0:T(1,128)S(1)} %pad_dynamic-slice_fusion.species_ref, bf16[128,32,128]{2,1,0:T(8,128)(2,1)} %all-to-all-done.1.got_ref), custom_call_target="tpu_custom_call" | custom-call | tf_op jit(solution)/shard_map/raster_steps/pallas_call | solution.py:147
  111.1 5.7 %all-to-all-start.2 = ((bf16[128,16,128]{2,1,0:T(8,128)(2,1)}), bf16[128,16,128]{2,1,0:T(8,128)(2,1)}, u32[]{:S(2)}, u32[]{:S(2)}) async-start(bf16[128,16,128]{2,1,0:T(8,128)(2,1)} %copy-done.12), calls=%async_computation.2 | async-start | bytes 1048576 | tf_op jit(solution)/shard_map/all_to_all | solution.py:455
  116.9 3.5 %reshape.155.index_ref = s32[4096,1]{1,0:T(8,128)} reshape(s32[128,32]{1,0:T(8,128)S(1)} %bitcast.69) | data formatting | bytes 32768 | tf_op jit(solution)/shard_map/jit(_where)/select_n | solution.py:431
  120.4 9.6 %all-to-all-done.2 = bf16[128,16,128]{2,1,0:T(8,128)(2,1)} async-done(((bf16[128,16,128]{2,1,0:T(8,128)(2,1)}), bf16[128,16,128]{2,1,0:T(8,128)(2,1)}, u32[]{:S(2)}, u32[]{:S(2)}) %all-to-all-start.2) | async-done | bytes 524320 | tf_op jit(solution)/shard_map/all_to_all | solution.py:455
  132.8 4.5 %pick_rows.2 = bf16[4096,128]{1,0:T(8,128)(2,1)S(1)} custom-call(s32[4096,1]{1,0:T(8,128)S(1)} %copy-done.4, bf16[128,2048]{1,0:T(8,128)(2,1)S(1)} %bitcast.56), custom_call_target="tpu_custom_call" | custom-call | tf_op jit(solution)/shard_map/pick_rows/pallas_call | solution.py:351
  137.3 23.7 %all_to_all.30 = bf16[128,32,128]{2,1,0:T(8,128)(2,1)} all-to-all(bf16[128,32,128]{2,1,0:T(8,128)(2,1)S(1)} %bitcast.55), channel_id=1, replica_groups=mesh['y'=4,'core'=2,'z'=4,'x'=4] {'y','core','z','x'}, dimensions={0} | all-to-all | bytes 2097152 | tf_op jit(solution)/shard_map/all_to_all | solution.py:458
  161.0 5.8 %all-to-all-start.4 = ((f32[128,16,128]{2,1,0:T(8,128)}), f32[128,16,128]{2,1,0:T(8,128)}, u32[]{:S(2)}, u32[]{:S(2)}) async-start(f32[128,16,128]{2,1,0:T(8,128)} %copy-done.11), calls=%async_computation.4 | async-start | bytes 2097152 | tf_op jit(solution)/shard_map/all_to_all | solution.py:466
  170.6 3.1 %pick_rows.3.dlog_own = bf16[2048,128]{1,0:T(8,128)(2,1)S(1)} custom-call(s32[2048,1]{1,0:T(8,128)S(1)} %copy-done.8, bf16[4096,128]{1,0:T(8,128)(2,1)S(1)} %bitcast.54, f32[2048,128]{1,0:T(8,128)S(1)} %land_forward.1.refs_0_), custom_call_target="tpu_custom_call" | custom-call | tf_op jit(solution)/shard_map/pick_rows/pallas_call | solution.py:351
  175.9 16.5 %land_backward.1 = f32[64,80,128]{2,1,0:T(8,128)} custom-call(s32[1]{0:T(128)} %bitcast.core_ref, bf16[2048,512]{1,0:T(8,128)(2,1)S(1)} %copy-done, bf16[2048,512]{1,0:T(8,128)(2,1)} %collective-permute-done.x_ref.x_other, bf16[2048,128]{1,0:T(8,128)(2,1)S(1)} %pick_rows.3.dlog_own, bf16[2048,128]{1,0:T(8,128)(2,1)S(1)} %collective-permute-done.1.dlog_other, ...), custom_call_target="tpu_custom_call" | custom-call | tf_op jit(solution)/shard_map/land_backward/pallas_call | solution.py:314
  192.5 10.0 %all-to-all-start.5 = ((f32[64,80,128]{2,1,0:T(8,128)}), f32[64,80,128]{2,1,0:T(8,128)S(1)}, u32[]{:S(2)}, u32[]{:S(2)}) async-start(f32[64,80,128]{2,1,0:T(8,128)} %land_backward.1), calls=%async_computation.5 | async-start | bytes 5242880 | tf_op jit(solution)/shard_map/all_to_all | solution.py:480
  202.5 2.5 %copy.95 = f32[16,8,16,128]{3,1,2,0:T(8,128)} copy(f32[16,8,16,128]{3,2,1,0:T(8,128)} %bitcast.33) | data formatting | bytes 2097152
  205.1 2.5 %copy.81 = f32[2048,128]{1,0:T(8,128)} copy(f32[2048,128]{0,1:T(8,128)} %bitcast.62) | data formatting | bytes 2097152 | tf_op jit(solution)/shard_map/transpose | solution.py:479
  207.6 31.9 %all-to-all-done.5 = f32[64,80,128]{2,1,0:T(8,128)S(1)} async-done(((f32[64,80,128]{2,1,0:T(8,128)}), f32[64,80,128]{2,1,0:T(8,128)S(1)}, u32[]{:S(2)}, u32[]{:S(2)}) %all-to-all-start.5) | async-done | bytes 2621472 | tf_op jit(solution)/shard_map/all_to_all | solution.py:480
  (90 shorter events, 36.1 us)
Async XLA Ops:
  0.6 3.5 %copy-start.16 = (s32[2048,1]{0,1:T(1,128)S(1)}, s32[2048,1]{0,1:T(1,128)}, u32[]{:S(2)}) copy-start(s32[2048,1]{0,1:T(1,128)} %param.18) | copy-start | bytes 24580
  0.6 3.5 %copy-start = (bf16[2048,512]{1,0:T(8,128)(2,1)S(1)}, bf16[2048,512]{1,0:T(8,128)(2,1)}, u32[]{:S(2)}) copy-start(bf16[2048,512]{1,0:T(8,128)(2,1)} %x_own.1) | copy-start | bytes 6291460
  0.7 3.5 %copy-start.1 = (bf16[512,2048]{1,0:T(8,128)(2,1)S(1)}, bf16[512,2048]{1,0:T(8,128)(2,1)}, u32[]{:S(2)}) copy-start(bf16[512,2048]{1,0:T(8,128)(2,1)} %w_in_ref.5) | copy-start | bytes 6291460
  0.7 3.5 %copy-start.9 = (bf16[2048,128]{1,0:T(8,128)(2,1)S(1)}, bf16[2048,128]{1,0:T(8,128)(2,1)}, u32[]{:S(2)}) copy-start(bf16[2048,128]{1,0:T(8,128)(2,1)} %w_out_ref.3) | copy-start | bytes 1572868
  0.7 3.5 %copy-start.13 = (f32[2048]{0:T(1024)S(1)}, f32[2048]{0:T(1024)}, u32[]{:S(2)}) copy-start(f32[2048]{0:T(1024)} %param.15) | copy-start | bytes 24580
  0.7 3.5 %copy-start.14 = (f32[128]{0:T(128)S(1)}, f32[128]{0:T(128)}, u32[]{:S(2)}) copy-start(f32[128]{0:T(128)} %param.17) | copy-start | bytes 1540
  13.6 4.2 %copy-start.20 = (s32[2048]{0:T(1024)S(1)}, s32[2048]{0:T(1024)}, u32[]{:S(2)}) copy-start(s32[2048]{0:T(1024)} %param.19) | copy-start | bytes 24580
  19.8 13.2 %copy-start.19 = (s32[16,128]{1,0:T(8,128)S(1)}, s32[16,128]{1,0:T(8,128)}, u32[]{:S(2)}) copy-start(s32[16,128]{1,0:T(8,128)} %param.25) | copy-start | bytes 24580
  21.1 33.0 %all-to-all-start = ((bf16[128,40,128]{2,1,0:T(8,128)(2,1)}), bf16[128,40,128]{2,1,0:T(8,128)(2,1)}, u32[]{:S(2)}, u32[]{:S(2)}) async-start(bf16[128,40,128]{2,1,0:T(8,128)(2,1)} %fusion.9), calls=%async_computation | async-start | bytes 2621440 | tf_op jit(solution)/shard_map/all_to_all | solution.py:424
  32.7 43.1 %collective-permute-start = (bf16[2048,512]{1,0:T(8,128)(2,1)S(1)}, bf16[2048,512]{1,0:T(8,128)(2,1)}, u32[]{:S(2)}, u32[]{:S(2)}) collective-permute-start(bf16[2048,512]{1,0:T(8,128)(2,1)S(1)} %copy-done), channel_id=1, source_target_pairs={{0,16},{16,0},{1,17},{17,1},{2,18},{18,2},{3,19},{19,3},{4,20},{20... | collective-permute-start | bytes 6291464 | tf_op jit(solution)/shard_map/ppermute | solution.py:367
  47.3 2.0 copy-start.5
  59.1 9.6 %copy-start.15 = (bf16[16,8,16,128]{3,2,1,0:T(8,128)(2,1)S(1)}, bf16[16,8,16,128]{3,2,1,0:T(8,128)(2,1)}, u32[]{:S(2)}) copy-start(bf16[16,8,16,128]{3,2,1,0:T(8,128)(2,1)} %copy.90) | copy-start | bytes 1572868
  67.6 7.9 %copy-start.18 = (f32[128,9]{0,1:T(8,128)S(1)}, f32[128,9]{0,1:T(8,128)}, u32[]{:S(2)}) copy-start(f32[128,9]{0,1:T(8,128)} %param.20) | copy-start | bytes 13828
  67.6 8.0 %copy-start.17 = (f32[128,9]{0,1:T(8,128)S(1)}, f32[128,9]{0,1:T(8,128)}, u32[]{:S(2)}) copy-start(f32[128,9]{0,1:T(8,128)} %param.21) | copy-start | bytes 13828
  67.6 8.0 %copy-start.21 = (f32[128]{0:T(128)S(1)}, f32[128]{0:T(128)}, u32[]{:S(2)}) copy-start(f32[128]{0:T(128)} %param.23) | copy-start | bytes 1540
  67.6 8.0 %copy-start.22 = (f32[128]{0:T(128)S(1)}, f32[128]{0:T(128)}, u32[]{:S(2)}) copy-start(f32[128]{0:T(128)} %param.22) | copy-start | bytes 1540
  69.6 24.4 %all-to-all-start.1 = ((bf16[128,32,128]{2,1,0:T(8,128)(2,1)}), bf16[128,32,128]{2,1,0:T(8,128)(2,1)}, u32[]{:S(2)}, u32[]{:S(2)}) async-start(bf16[128,32,128]{2,1,0:T(8,128)(2,1)} %constant_dynamic-update-slice_fusion), calls=%async_computation.1 | async-start | bytes 2097152 | tf_op jit(solution)/shard_map/all_to_all | solution.py:450
  85.2 2.0 copy-start.6
  111.1 18.9 %all-to-all-start.2 = ((bf16[128,16,128]{2,1,0:T(8,128)(2,1)}), bf16[128,16,128]{2,1,0:T(8,128)(2,1)}, u32[]{:S(2)}, u32[]{:S(2)}) async-start(bf16[128,16,128]{2,1,0:T(8,128)(2,1)} %copy-done.12), calls=%async_computation.2 | async-start | bytes 1048576 | tf_op jit(solution)/shard_map/all_to_all | solution.py:455
  161.0 31.5 %all-to-all-start.4 = ((f32[128,16,128]{2,1,0:T(8,128)}), f32[128,16,128]{2,1,0:T(8,128)}, u32[]{:S(2)}, u32[]{:S(2)}) async-start(f32[128,16,128]{2,1,0:T(8,128)} %copy-done.11), calls=%async_computation.4 | async-start | bytes 2097152 | tf_op jit(solution)/shard_map/all_to_all | solution.py:466
  170.6 5.3 %copy-start.10 = (bf16[2048,128]{1,0:T(8,128)(2,1)S(1)}, bf16[2048,128]{1,0:T(8,128)(2,1)}, u32[]{:S(2)}) copy-start(bf16[2048,128]{1,0:T(8,128)(2,1)} %w_out_ref.3) | copy-start | bytes 1572868
  173.7 2.3 collective-permute-start.1
  192.5 47.0 %all-to-all-start.5 = ((f32[64,80,128]{2,1,0:T(8,128)}), f32[64,80,128]{2,1,0:T(8,128)S(1)}, u32[]{:S(2)}, u32[]{:S(2)}) async-start(f32[64,80,128]{2,1,0:T(8,128)} %land_backward.1), calls=%async_computation.5 | async-start | bytes 5242880 | tf_op jit(solution)/shard_map/all_to_all | solution.py:480
  239.7 1.3 collective-permute-start.2
  (7 other events, 9.0 us)
where the time goes:
time: 244 us; the launch traced here: 242 us
  Pallas kernels  62.4 us (26%)
  waiting for transfers between devices  55.6 us (23%)
  starting transfers between devices  39.8 us (16%)
  local copies, waits for them, and re-layouts  35.5 us (15%)
  blocking collectives  23.7 us (10%)
  matrix products  15.5 us (6%)
  other arithmetic  7.88 us (3%)
    all_to_all x1, waiting for transfers between devices, local(): pieces = lax.all_to_all(pieces, ('y', 'z', 'x'), 0, 0)  31.9 us
    all_to_all x1, blocking collectives, local(): lax.all_to_all(back_values.reshape(devices, slot_count, species), ALL, sp...  23.7 us
    unnamed x52, local copies, waits for them, and re-layouts  19.8 us
    pallas_call x1, Pallas kernels, backward(): pl.pallas_call(backward_body, out_shape=jax.ShapeDtypeStruct((peers, send...  16.5 us
    pallas_call x1, Pallas kernels, raster(): pl.pallas_call(functools.partial(raster_body, scale), out_shape=[jax.Shap...  15.4 us
    pallas_call x2, Pallas kernels, gates(): pl.pallas_call(gates_body, out_shape=[jax.ShapeDtypeStruct((rows, hid //...  14.1 us
    all_to_all x1, starting transfers between devices, local(): got = lax.all_to_all(send, ALL, split_axis=0, concat_axis=0, tiled=True)  11.6 us
    all_to_all x1, starting transfers between devices, local(): pieces = lax.all_to_all(pieces, ('y', 'z', 'x'), 0, 0)  10 us
  transfers between devices with their start and end apart: 8, of which 6 were waited for; matrix products, arithmetic and copies ran while one was open for 13% of the time, Pallas kernels for 14%

commit v1 on v0

--- a/solution.py
+++ b/solution.py
@@ -320,10 +320,75 @@
     )(core, *x, *dlog, *hidden, *slope, w_out)
 
 
+def place_body(slot_count, got_ref, code_ref, out_ref, total):
+    sources, _, species = got_ref.shape
+    tall, wide = code_ref.shape[1:]
+    half = tall // 2
+    keys = half * wide
+    group = 4
+    values = jnp.swapaxes(got_ref[:, :slot_count, :].astype(F32), 0, 1).astype(BF16)
+    spots = got_ref[:, slot_count : slot_count + 8, :].astype(F32)[:, 0, :]
+    along = spots.T
+    ids = lax.broadcasted_iota(jnp.int32, (keys, sources), 0)
+    for first in range(0, slot_count, group):
+        hots, rows = [], []
+        for slot in range(first, first + group):
+            row = along[slot : slot + 1, :].astype(jnp.int32) - 1
+            col = along[slot_count + slot : slot_count + slot + 1, :].astype(jnp.int32)
+            cell = row * wide + col
+            key = jnp.where(row >= half, cell - keys, cell)
+            hots.append(jnp.where(ids == key, 1.0, 0.0).astype(BF16))
+            upper = spots[:, slot : slot + 1] > half
+            value = values[slot].astype(F32)
+            rows.append(
+                jnp.concatenate(
+                    [jnp.where(upper, 0.0, value), jnp.where(upper, value, 0.0)], axis=1
+                ).astype(BF16)
+            )
+        part = jnp.dot(
+            jnp.concatenate(hots, axis=1),
+            jnp.concatenate(rows, axis=0),
+            preferred_element_type=F32,
+        )
+        if first == 0:
+            total[...] = part
+        else:
+            total[...] += part
+    lines = [
+        total[
+            r % half * wide : (r % half + 1) * wide,
+            r // half * species : (r // half + 1) * species,
+        ].T
+        for r in range(tall)
+    ]
+    out_ref[:, :tall, :] = jnp.swapaxes(jnp.stack(lines), 0, 1).astype(BF16)
+    out_ref[:, tall:, :] = code_ref[...]
+
+
+def place(got, code, slot_count):
+    _, tall, wide = code.shape
+    species = got.shape[2]
+
+    def whole(shape):
+        return pl.BlockSpec(shape, lambda: (0,) * len(shape))
+
+    return pl.pallas_call(
+        functools.partial(place_body, slot_count),
+        out_shape=jax.ShapeDtypeStruct((species, 2 * tall, wide), BF16),
+        in_specs=[whole(got.shape), whole(code.shape)],
+        out_specs=whole((species, 2 * tall, wide)),
+        scratch_shapes=[pltpu.VMEM((tall * wide // 2, 2 * species), F32)],
+        compiler_params=pltpu.CompilerParams(vmem_limit_bytes=40 << 20),
+        name="place_cells",
+    )(got, code)
+
+
 def pick_body(wide, index_ref, table_ref, *refs):
+    out_ref = refs[-1]
+    rows, lanes = out_ref.shape
     index = index_ref[...]
-    out_ref = refs[-1]
-    lanes = out_ref.shape[1]
+    if index.shape[1] != 1:
+        index = jnp.broadcast_to(index, (8, rows)).T[:, :1]
     if wide:
         keys = table_ref.shape[1] // 2
         table = jnp.concatenate([table_ref[:, :keys], table_ref[:, keys:]], axis=0)
@@ -344,7 +409,8 @@
 
 
 def pick(index, table, factors=None, wide=False, block=512):
-    rows = index.shape[0]
+    rows = index.size
+    column = index.shape[1] == 1
     lanes = table.shape[0] if wide else table.shape[1]
     block_spec = pl.BlockSpec((block, lanes), lambda i: (i, 0))
     more = () if factors is None else (factors,)
@@ -353,14 +419,16 @@
         out_shape=jax.ShapeDtypeStruct((rows, lanes), BF16),
         grid=(rows // block,),
         in_specs=[
-            pl.BlockSpec((block, 1), lambda i: (i, 0)),
+            pl.BlockSpec((block, 1), lambda i: (i, 0))
+            if column
+            else pl.BlockSpec((1, block), lambda i: (0, i)),
             pl.BlockSpec(table.shape, lambda i: (0, 0), pipeline_mode=pl.Buffered(1)),
         ]
         + [block_spec] * len(more),
         out_specs=block_spec,
         compiler_params=pltpu.CompilerParams(vmem_limit_bytes=40 << 20),
         name="pick_rows",
-    )(index[:, None], table, *more)
+    )(index, table, *more)
 
 
 def other_core(values):
@@ -425,22 +493,13 @@
     send, own = lax.optimization_barrier((send, covariates))
     own_gates = gates(core[None], own, w_in, b_in)
     got, own_gates = lax.optimization_barrier((got, own_gates))
-    got_values = got[:, :slot_count].reshape(slots, species)
     got_row = got[:, slot_count, :slot_count].astype(jnp.int32)
     got_col = got[:, slot_count, slot_count : 2 * slot_count].astype(jnp.int32)
     cell_list = jnp.where(got_row > 0, (got_row - 1) * tile_width + got_col, -1).reshape(-1)
-    cell_ids = jnp.arange(cell_count, dtype=jnp.int32)
-    place = (cell_list[None, :] == cell_ids[:, None]).astype(BF16)
-    start_field = jnp.dot(place, got_values, preferred_element_type=F32)
 
     code = jnp.where(surveyed[:, :, None] > 0, observed, -1).astype(BF16)
-    send = jnp.concatenate(
-        [
-            start_field.astype(BF16).T.reshape(species, height, tile_width),
-            code.reshape(cell_count, species).T.reshape(species, height, tile_width),
-        ],
-        axis=1,
-    )
+    code = code.reshape(cell_count, species).T.reshape(species, height, tile_width)
+    send = place(got, code, slot_count)
     traits = jnp.concatenate(
         [normalize(row_taps), normalize(col_taps), rate[:, None], capacity[:, None]], axis=1
     )
@@ -454,7 +513,7 @@
     density, grad_start = raster(traits, got, scale, tiles_y, tiles_x)
     grad_start = lax.all_to_all(grad_start, ALL, 0, 0, tiled=True).reshape(species, cell_count)
 
-    back_values = pick(cell_list, grad_start, wide=True)
+    back_values = pick(cell_list[:, None], grad_start, wide=True)
     home_values = lax.all_to_all(
         back_values.reshape(devices, slot_count, species),
         ALL,
@@ -464,7 +523,7 @@
     )
     home_values, density = lax.optimization_barrier((home_values, density))
     density = lax.all_to_all(density, ALL, 0, 0, tiled=True)
-    dlog = pick(flat_slot, home_values.reshape(slots, species), intensity)
+    dlog = pick(flat_slot[None, :], home_values.reshape(slots, species), intensity)
     peers = devices // 2
     pieces = backward(
         core[None],

time: 244 us -> 235 us (0.963)
  matrix products: 15.5 us -> 7.04 us
  Pallas kernels: 62.4 us -> 69.8 us
  local copies, waits for them, and re-layouts: 35.5 us -> 30.2 us
    dot_general x1 -> x0, matrix products: 8.49 us -> none  [local(): start_field = jnp.dot(place, got_values, preferred_element_type=F32)]
    pallas_call x0 -> x1, Pallas kernels: none -> 6.6 us  [place(): pl.pallas_call(functools.partial(place_body, slot_count), out_shape=jax.S...]
    unnamed x52 -> x49, local copies, waits for them, and re-layouts: 19.8 us -> 19.4 us
  transfers between devices with their start and end apart: 8 -> 8, of which waited for: 6 -> 6; matrix products, arithmetic and copies ran while one was open for 13% -> 7% of each run, Pallas kernels for 14% -> 18%
where the time goes in v1:
time: 235 us; the launch traced here: 233 us
  Pallas kernels  69.8 us (30%)
  waiting for transfers between devices  54.2 us (23%)
  starting transfers between devices  39.8 us (17%)
  local copies, waits for them, and re-layouts  30.2 us (13%)
  blocking collectives  23.7 us (10%)
  other arithmetic  7.19 us (3%)
  matrix products  7.04 us (3%)
    all_to_all x1, waiting for transfers between devices, local(): pieces = lax.all_to_all(pieces, ('y', 'z', 'x'), 0, 0)  31.9 us
    all_to_all x1, blocking collectives, local(): lax.all_to_all(back_values.reshape(devices, slot_count, species), ALL, sp...  23.7 us
    unnamed x49, local copies, waits for them, and re-layouts  19.4 us
    pallas_call x1, Pallas kernels, backward(): pl.pallas_call(backward_body, out_shape=jax.ShapeDtypeStruct((peers, send...  16.5 us
    pallas_call x1, Pallas kernels, raster(): pl.pallas_call(functools.partial(raster_body, scale), out_shape=[jax.Shap...  15.4 us
    pallas_call x2, Pallas kernels, gates(): pl.pallas_call(gates_body, out_shape=[jax.ShapeDtypeStruct((rows, hid //...  14.1 us
    all_to_all x1, starting transfers between devices, local(): got = lax.all_to_all(send, ALL, split_axis=0, concat_axis=0, tiled=True)  11.6 us
    all_to_all x1, starting transfers between devices, local(): pieces = lax.all_to_all(pieces, ('y', 'z', 'x'), 0, 0)  10 us
  transfers between devices with their start and end apart: 8, of which 6 were waited for; matrix products, arithmetic and copies ran while one was open for 7% of the time, Pallas kernels for 18%

profile of v1, /device:TPU:0, one launch (start us, length us, event | category | flops | bytes accessed | tf_op | source)
XLA Modules:
  0.0 233.0 jit_solution(1969620636312173341)
XLA Ops:
  0.7 3.4 %fusion.7 = f32[2048]{0:T(1024)S(1)} fusion(s32[2048]{0:T(1024)} %bitcast.68), kind=kOutput, calls=%fused_computation.10 | convolution fusion | flops 1078982656 | bytes 16384 | tf_op jit(solution)/shard_map/dot_general | solution.py:469
  4.2 8.9 %land_forward.1.refs_0_ = f32[2048,128]{1,0:T(8,128)S(1)} custom-call(bf16[2048,512]{1,0:T(8,128)(2,1)S(1)} %copy-done, bf16[512,2048]{1,0:T(8,128)(2,1)S(1)} %copy-done.1, f32[1,2048]{1,0:T(1,128)S(1)} %bitcast.55, bf16[2048,128]{1,0:T(8,128)(2,1)S(1)} %copy-done.9, f32[1,128]{1,0:T(1,128)S(1)} %bitcast.58), custom_call_target="tpu_custom_call" | custom-call | tf_op jit(solution)/shard_map/land_forward/pallas_call | solution.py:186
  13.6 3.2 %fusion.4 = bf16[2048,256]{1,0:T(8,128)(2,1)S(1)} fusion(s32[2048]{0:T(1024)S(1)} %compare_select_fusion.1, bf16[2048,128]{1,0:T(8,128)(2,1)S(1)} %get-tuple-element.44, bf16[2048,128]{1,0:T(8,128)(2,1)S(1)} %get-tuple-element.43), kind=kOutput, calls=%fused_computation.7 | convolution fusion | flops 2154299392 | bytes 2105344 | tf_op jit(solution)/shard_map/dot_general | solution.py:481
  21.1 11.6 %all-to-all-start = ((bf16[128,40,128]{2,1,0:T(8,128)(2,1)}), bf16[128,40,128]{2,1,0:T(8,128)(2,1)}, u32[]{:S(2)}, u32[]{:S(2)}) async-start(bf16[128,40,128]{2,1,0:T(8,128)(2,1)} %fusion.6), calls=%async_computation | async-start | bytes 2621440 | tf_op jit(solution)/shard_map/all_to_all | solution.py:492
  33.0 2.4 %select_convert_fusion = bf16[16,128,128]{2,1,0:T(8,128)(2,1)} fusion(s32[16,128,128]{2,1,0:T(8,128)} %param.24, pred[16,128]{1,0:T(8,128)(4,1)S(1)} %broadcast_compare_fusion), kind=kLoop, calls=%fused_computation.18 | loop fusion | flops 524288 | bytes 1574912 | tf_op jit(solution)/shard_map/convert_element_type | solution.py:500
  41.0 6.3 %land_gates.2 = (bf16[2048,1024]{1,0:T(8,128)(2,1)S(1)}, f32[2048,1024]{1,0:T(8,128)}) custom-call(s32[1]{0:T(128)} %bitcast.core_ref, bf16[2048,512]{1,0:T(8,128)(2,1)S(1)} %copy-done, bf16[512,2048]{1,0:T(8,128)(2,1)S(1)} %copy-done.2, f32[1,2048]{1,0:T(1,128)S(1)} %bitcast.56), custom_call_target="tpu_custom_call" | custom-call | tf_op jit(solution)/shard_map/land_gates/pallas_call | solution.py:217
  49.2 4.9 %all-to-all-done.got_ref = bf16[128,40,128]{2,1,0:T(8,128)(2,1)} async-done(((bf16[128,40,128]{2,1,0:T(8,128)(2,1)}), bf16[128,40,128]{2,1,0:T(8,128)(2,1)}, u32[]{:S(2)}, u32[]{:S(2)}) %all-to-all-start) | async-done | bytes 1310752 | tf_op jit(solution)/shard_map/all_to_all | solution.py:492
  55.1 6.6 %place_cells.1 = bf16[128,32,128]{2,1,0:T(8,128)(2,1)S(1)} custom-call(bf16[128,40,128]{2,1,0:T(8,128)(2,1)} %all-to-all-done.got_ref, bf16[128,16,128]{2,1,0:T(8,128)(2,1)S(1)} %bitcast.54), custom_call_target="tpu_custom_call" | custom-call | tf_op jit(solution)/shard_map/place_cells/pallas_call | solution.py:375
  62.7 6.0 %all-to-all-start.1 = ((bf16[128,32,128]{2,1,0:T(8,128)(2,1)}), bf16[128,32,128]{2,1,0:T(8,128)(2,1)}, u32[]{:S(2)}, u32[]{:S(2)}) async-start(bf16[128,32,128]{2,1,0:T(8,128)(2,1)} %copy-done.8), calls=%async_computation.1 | async-start | bytes 2097152 | tf_op jit(solution)/shard_map/all_to_all | solution.py:509
  70.6 7.8 %land_gates.3 = (bf16[2048,1024]{1,0:T(8,128)(2,1)S(1)}, f32[2048,1024]{1,0:T(8,128)}) custom-call(s32[1]{0:T(128)} %bitcast.core_ref, bf16[2048,512]{1,0:T(8,128)(2,1)} %collective-permute-done.x_ref.x_other, bf16[512,2048]{1,0:T(8,128)(2,1)S(1)} %copy-done.3, f32[1,2048]{1,0:T(1,128)S(1)} %bitcast.57), custom_call_target="tpu_custom_call" | custom-call | tf_op jit(solution)/shard_map/land_gates/pallas_call | solution.py:217
  80.3 6.8 %all-to-all-done.1.got_ref = bf16[128,32,128]{2,1,0:T(8,128)(2,1)} async-done(((bf16[128,32,128]{2,1,0:T(8,128)(2,1)}), bf16[128,32,128]{2,1,0:T(8,128)(2,1)}, u32[]{:S(2)}, u32[]{:S(2)}) %all-to-all-start.1) | async-done | bytes 1048608 | tf_op jit(solution)/shard_map/all_to_all | solution.py:509
  87.1 15.4 %raster_steps.1 = (f32[128,16,128]{2,1,0:T(8,128)S(1)}, bf16[128,16,128]{2,1,0:T(8,128)(2,1)S(1)}) custom-call(f32[1,32]{1,0:T(1,128)S(1)} %pad_dynamic-slice_fusion.species_ref, bf16[128,32,128]{2,1,0:T(8,128)(2,1)} %all-to-all-done.1.got_ref), custom_call_target="tpu_custom_call" | custom-call | tf_op jit(solution)/shard_map/raster_steps/pallas_call | solution.py:147
  104.3 5.7 %all-to-all-start.2 = ((bf16[128,16,128]{2,1,0:T(8,128)(2,1)}), bf16[128,16,128]{2,1,0:T(8,128)(2,1)}, u32[]{:S(2)}, u32[]{:S(2)}) async-start(bf16[128,16,128]{2,1,0:T(8,128)(2,1)} %copy-done.13), calls=%async_computation.2 | async-start | bytes 1048576 | tf_op jit(solution)/shard_map/all_to_all | solution.py:514
  111.5 3.6 %reshape.139.index_ref = s32[4096,1]{1,0:T(8,128)} reshape(s32[128,32]{1,0:T(8,128)S(1)} %fusion.17) | data formatting | bytes 32768 | tf_op jit(solution)/shard_map/jit(_where)/select_n | solution.py:498
  115.0 8.2 %all-to-all-done.2 = bf16[128,16,128]{2,1,0:T(8,128)(2,1)} async-done(((bf16[128,16,128]{2,1,0:T(8,128)(2,1)}), bf16[128,16,128]{2,1,0:T(8,128)(2,1)}, u32[]{:S(2)}, u32[]{:S(2)}) %all-to-all-start.2) | async-done | bytes 524320 | tf_op jit(solution)/shard_map/all_to_all | solution.py:514
  126.0 4.5 %pick_rows.2 = bf16[4096,128]{1,0:T(8,128)(2,1)S(1)} custom-call(s32[4096,1]{1,0:T(8,128)S(1)} %copy-done.4, bf16[128,2048]{1,0:T(8,128)(2,1)S(1)} %bitcast.53), custom_call_target="tpu_custom_call" | custom-call | tf_op jit(solution)/shard_map/pick_rows/pallas_call | solution.py:417
  130.4 23.7 %all_to_all.30 = bf16[128,32,128]{2,1,0:T(8,128)(2,1)} all-to-all(bf16[128,32,128]{2,1,0:T(8,128)(2,1)S(1)} %bitcast.51), channel_id=1, replica_groups=mesh['y'=4,'core'=2,'z'=4,'x'=4] {'y','core','z','x'}, dimensions={0} | all-to-all | bytes 2097152 | tf_op jit(solution)/shard_map/all_to_all | solution.py:517
  154.1 5.8 %all-to-all-start.4 = ((f32[128,16,128]{2,1,0:T(8,128)}), f32[128,16,128]{2,1,0:T(8,128)}, u32[]{:S(2)}, u32[]{:S(2)}) async-start(f32[128,16,128]{2,1,0:T(8,128)} %copy-done.12), calls=%async_computation.4 | async-start | bytes 2097152 | tf_op jit(solution)/shard_map/all_to_all | solution.py:525
  161.2 3.9 %pick_rows.3.dlog_own = bf16[2048,128]{1,0:T(8,128)(2,1)S(1)} custom-call(s32[1,2048]{1,0:T(1,128)S(1)} %bitcast_add_fusion.index_ref, bf16[4096,128]{1,0:T(8,128)(2,1)S(1)} %bitcast.52, f32[2048,128]{1,0:T(8,128)S(1)} %land_forward.1.refs_0_), custom_call_target="tpu_custom_call" | custom-call | tf_op jit(solution)/shard_map/pick_rows/pallas_call | solution.py:417
  167.3 16.5 %land_backward.1 = f32[64,80,128]{2,1,0:T(8,128)} custom-call(s32[1]{0:T(128)} %bitcast.core_ref, bf16[2048,512]{1,0:T(8,128)(2,1)S(1)} %copy-done, bf16[2048,512]{1,0:T(8,128)(2,1)} %collective-permute-done.x_ref.x_other, bf16[2048,128]{1,0:T(8,128)(2,1)S(1)} %pick_rows.3.dlog_own, bf16[2048,128]{1,0:T(8,128)(2,1)S(1)} %collective-permute-done.1.dlog_other, ...), custom_call_target="tpu_custom_call" | custom-call | tf_op jit(solution)/shard_map/land_backward/pallas_call | solution.py:314
  183.9 10.0 %all-to-all-start.5 = ((f32[64,80,128]{2,1,0:T(8,128)}), f32[64,80,128]{2,1,0:T(8,128)S(1)}, u32[]{:S(2)}, u32[]{:S(2)}) async-start(f32[64,80,128]{2,1,0:T(8,128)} %land_backward.1), calls=%async_computation.5 | async-start | bytes 5242880 | tf_op jit(solution)/shard_map/all_to_all | solution.py:539
  193.9 2.5 %copy.71 = f32[16,8,16,128]{3,1,2,0:T(8,128)} copy(f32[16,8,16,128]{3,2,1,0:T(8,128)} %bitcast.31) | data formatting | bytes 2097152
  196.5 2.5 %copy.59 = f32[2048,128]{1,0:T(8,128)} copy(f32[2048,128]{0,1:T(8,128)} %bitcast.60) | data formatting | bytes 2097152 | tf_op jit(solution)/shard_map/transpose | solution.py:538
  199.0 31.9 %all-to-all-done.5 = f32[64,80,128]{2,1,0:T(8,128)S(1)} async-done(((f32[64,80,128]{2,1,0:T(8,128)}), f32[64,80,128]{2,1,0:T(8,128)S(1)}, u32[]{:S(2)}, u32[]{:S(2)}) %all-to-all-start.5) | async-done | bytes 2621472 | tf_op jit(solution)/shard_map/all_to_all | solution.py:539
  (84 shorter events, 30.0 us)
Async XLA Ops:
  0.6 3.5 %copy-start.16 = (s32[2048,1]{0,1:T(1,128)S(1)}, s32[2048,1]{0,1:T(1,128)}, u32[]{:S(2)}) copy-start(s32[2048,1]{0,1:T(1,128)} %param.18) | copy-start | bytes 24580
  0.6 3.5 %copy-start = (bf16[2048,512]{1,0:T(8,128)(2,1)S(1)}, bf16[2048,512]{1,0:T(8,128)(2,1)}, u32[]{:S(2)}) copy-start(bf16[2048,512]{1,0:T(8,128)(2,1)} %x_own.1) | copy-start | bytes 6291460
  0.7 3.5 %copy-start.1 = (bf16[512,2048]{1,0:T(8,128)(2,1)S(1)}, bf16[512,2048]{1,0:T(8,128)(2,1)}, u32[]{:S(2)}) copy-start(bf16[512,2048]{1,0:T(8,128)(2,1)} %w_in_ref.5) | copy-start | bytes 6291460
  0.7 3.5 %copy-start.9 = (bf16[2048,128]{1,0:T(8,128)(2,1)S(1)}, bf16[2048,128]{1,0:T(8,128)(2,1)}, u32[]{:S(2)}) copy-start(bf16[2048,128]{1,0:T(8,128)(2,1)} %w_out_ref.3) | copy-start | bytes 1572868
  0.7 3.5 %copy-start.14 = (f32[2048]{0:T(1024)S(1)}, f32[2048]{0:T(1024)}, u32[]{:S(2)}) copy-start(f32[2048]{0:T(1024)} %param.15) | copy-start | bytes 24580
  0.7 3.5 %copy-start.15 = (f32[128]{0:T(128)S(1)}, f32[128]{0:T(128)}, u32[]{:S(2)}) copy-start(f32[128]{0:T(128)} %param.17) | copy-start | bytes 1540
  13.5 4.2 %copy-start.20 = (s32[2048]{0:T(1024)S(1)}, s32[2048]{0:T(1024)}, u32[]{:S(2)}) copy-start(s32[2048]{0:T(1024)} %param.19) | copy-start | bytes 24580
  19.8 13.2 %copy-start.19 = (s32[16,128]{1,0:T(8,128)S(1)}, s32[16,128]{1,0:T(8,128)}, u32[]{:S(2)}) copy-start(s32[16,128]{1,0:T(8,128)} %param.25) | copy-start | bytes 24580
  21.1 33.0 %all-to-all-start = ((bf16[128,40,128]{2,1,0:T(8,128)(2,1)}), bf16[128,40,128]{2,1,0:T(8,128)(2,1)}, u32[]{:S(2)}, u32[]{:S(2)}) async-start(bf16[128,40,128]{2,1,0:T(8,128)(2,1)} %fusion.6), calls=%async_computation | async-start | bytes 2621440 | tf_op jit(solution)/shard_map/all_to_all | solution.py:492
  32.7 36.3 %collective-permute-start = (bf16[2048,512]{1,0:T(8,128)(2,1)S(1)}, bf16[2048,512]{1,0:T(8,128)(2,1)}, u32[]{:S(2)}, u32[]{:S(2)}) collective-permute-start(bf16[2048,512]{1,0:T(8,128)(2,1)S(1)} %copy-done), channel_id=1, source_target_pairs={{0,16},{16,0},{1,17},{17,1},{2,18},{18,2},{3,19},{19,3},{4,20},{20... | collective-permute-start | bytes 6291464 | tf_op jit(solution)/shard_map/ppermute | solution.py:435
  41.0 27.8 %copy-start.18 = (f32[128,9]{0,1:T(8,128)S(1)}, f32[128,9]{0,1:T(8,128)}, u32[]{:S(2)}) copy-start(f32[128,9]{0,1:T(8,128)} %param.20) | copy-start | bytes 13828
  41.0 27.8 %copy-start.17 = (f32[128,9]{0,1:T(8,128)S(1)}, f32[128,9]{0,1:T(8,128)}, u32[]{:S(2)}) copy-start(f32[128,9]{0,1:T(8,128)} %param.21) | copy-start | bytes 13828
  47.3 1.9 copy-start.5
  49.2 19.6 %copy-start.21 = (f32[128]{0:T(128)S(1)}, f32[128]{0:T(128)}, u32[]{:S(2)}) copy-start(f32[128]{0:T(128)} %param.23) | copy-start | bytes 1540
  49.2 19.6 %copy-start.22 = (f32[128]{0:T(128)S(1)}, f32[128]{0:T(128)}, u32[]{:S(2)}) copy-start(f32[128]{0:T(128)} %param.22) | copy-start | bytes 1540
  62.7 24.4 %all-to-all-start.1 = ((bf16[128,32,128]{2,1,0:T(8,128)(2,1)}), bf16[128,32,128]{2,1,0:T(8,128)(2,1)}, u32[]{:S(2)}, u32[]{:S(2)}) async-start(bf16[128,32,128]{2,1,0:T(8,128)(2,1)} %copy-done.8), calls=%async_computation.1 | async-start | bytes 2097152 | tf_op jit(solution)/shard_map/all_to_all | solution.py:509
  69.0 1.6 copy-start.3
  78.3 2.0 copy-start.6
  104.3 18.9 %all-to-all-start.2 = ((bf16[128,16,128]{2,1,0:T(8,128)(2,1)}), bf16[128,16,128]{2,1,0:T(8,128)(2,1)}, u32[]{:S(2)}, u32[]{:S(2)}) async-start(bf16[128,16,128]{2,1,0:T(8,128)(2,1)} %copy-done.13), calls=%async_computation.2 | async-start | bytes 1048576 | tf_op jit(solution)/shard_map/all_to_all | solution.py:514
  154.1 29.7 %all-to-all-start.4 = ((f32[128,16,128]{2,1,0:T(8,128)}), f32[128,16,128]{2,1,0:T(8,128)}, u32[]{:S(2)}, u32[]{:S(2)}) async-start(f32[128,16,128]{2,1,0:T(8,128)} %copy-done.12), calls=%async_computation.4 | async-start | bytes 2097152 | tf_op jit(solution)/shard_map/all_to_all | solution.py:525
  161.2 6.2 %copy-start.10 = (bf16[2048,128]{1,0:T(8,128)(2,1)S(1)}, bf16[2048,128]{1,0:T(8,128)(2,1)}, u32[]{:S(2)}) copy-start(bf16[2048,128]{1,0:T(8,128)(2,1)} %w_out_ref.3) | copy-start | bytes 1572868
  165.1 2.3 collective-permute-start.1
  183.9 47.0 %all-to-all-start.5 = ((f32[64,80,128]{2,1,0:T(8,128)}), f32[64,80,128]{2,1,0:T(8,128)S(1)}, u32[]{:S(2)}, u32[]{:S(2)}) async-start(f32[64,80,128]{2,1,0:T(8,128)} %land_backward.1), calls=%async_computation.5 | async-start | bytes 5242880 | tf_op jit(solution)/shard_map/all_to_all | solution.py:539
  231.1 1.3 collective-permute-start.2
  (7 other events, 8.2 us)

commit v2 on v1

--- a/solution.py
+++ b/solution.py
@@ -318,6 +318,81 @@
         compiler_params=pltpu.CompilerParams(vmem_limit_bytes=50 << 20),
         name="land_backward",
     )(core, *x, *dlog, *hidden, *slope, w_out)
+
+
+def pack_body(wide, owner_ref, cell_ref, intensity_ref, send_ref, slot_ref):
+    devices, tall, species = send_ref.shape
+    slot_count = tall - 8
+    rows = intensity_ref.shape[0]
+    half = devices * slot_count // 2
+    block = 256
+    owner = owner_ref[...]
+    hot = jnp.where(lax.broadcasted_iota(jnp.int32, (devices, rows), 0) == owner, 1.0, 0.0)
+    first = lax.broadcasted_iota(jnp.int32, (block, block), 0)
+    second = lax.broadcasted_iota(jnp.int32, (block, block), 1)
+    earlier = jnp.where(first < second, 1.0, 0.0).astype(BF16)
+    count = jnp.zeros((devices, 1), F32)
+    parts = []
+    for at in range(0, rows, block):
+        here = hot[:, at : at + block]
+        before = jnp.dot(here.astype(BF16), earlier, preferred_element_type=F32) + count
+        parts.append(jnp.sum(before * here, axis=0, keepdims=True))
+        count = count + jnp.sum(here, axis=1, keepdims=True)
+    slot = jnp.concatenate(parts, axis=1).astype(jnp.int32)
+    flat = owner * slot_count + slot
+    slot_ref[...] = flat
+
+    cell = cell_ref[...].astype(F32)
+    row = jnp.floor(cell / wide)
+    col = cell - row * wide
+    taken = lax.broadcasted_iota(jnp.int32, (slot_count, rows), 0) == slot
+    places = jnp.concatenate(
+        [jnp.where(taken, row + 1.0, 0.0), jnp.where(taken, col, 0.0)], axis=0
+    ).astype(BF16)
+    table = lax.dot_general(
+        places, hot.astype(BF16), (((1,), (1,)), ((), ())), preferred_element_type=F32
+    ).T
+    table = jnp.concatenate([table, jnp.zeros((devices, species - 2 * slot_count), F32)], axis=1)
+    line = lax.broadcasted_iota(jnp.int32, (devices, 8, species), 1)
+    send_ref[:, slot_count:, :] = jnp.where(line == 0, table[:, None, :], 0.0).astype(BF16)
+
+    key = jnp.where(flat >= half, flat - half, flat)
+    upper = jnp.broadcast_to(flat, (8, rows)).T[:, :1] >= half
+    value = intensity_ref[...]
+    value = jnp.concatenate(
+        [jnp.where(upper, 0.0, value), jnp.where(upper, value, 0.0)], axis=1
+    ).astype(BF16)
+    step = 16 * slot_count
+    ids = lax.broadcasted_iota(jnp.int32, (step, rows), 0)
+    for at in range(0, half, step):
+        pick = jnp.where(ids == key - at, 1.0, 0.0).astype(BF16)
+        out = jnp.dot(pick, value, preferred_element_type=F32)
+        for side in range(2):
+            to = (side * half + at) // slot_count
+            send_ref[to : to + 16, :slot_count, :] = (
+                out[:, side * species : (side + 1) * species]
+                .reshape(16, slot_count, species)
+                .astype(BF16)
+            )
+
+
+def pack(owner, cell, intensity, devices, slot_count, wide):
+    rows, species = intensity.shape
+
+    def whole(shape):
+        return pl.BlockSpec(shape, lambda: (0,) * len(shape))
+
+    return pl.pallas_call(
+        functools.partial(pack_body, wide),
+        out_shape=[
+            jax.ShapeDtypeStruct((devices, slot_count + 8, species), BF16),
+            jax.ShapeDtypeStruct((1, rows), jnp.int32),
+        ],
+        in_specs=[whole((1, rows)), whole((1, rows)), whole((rows, species))],
+        out_specs=[whole((devices, slot_count + 8, species)), whole((1, rows))],
+        compiler_params=pltpu.CompilerParams(vmem_limit_bytes=48 << 20),
+        name="pack_cells",
+    )(owner, cell, intensity)
 
 
 def place_body(slot_count, got_ref, code_ref, out_ref, total):
@@ -462,33 +537,14 @@
     theirs = other_core(covariates)
     intensity = forward(covariates, w_in, b_in, w_out, b_out)
 
-    owner_rows = owner[:, 0]
-    owner_hot = owner_rows[:, None] == jnp.arange(devices, dtype=jnp.int32)[None, :]
-    row_ids = jnp.arange(row_count, dtype=jnp.int32)
-    earlier = (row_ids[None, :] < row_ids[:, None]).astype(BF16)
-    before = jnp.dot(earlier, owner_hot.astype(BF16), preferred_element_type=F32)
-    slot_idx = jnp.sum(jnp.where(owner_hot, before, 0.0), axis=1).astype(jnp.int32)
-    flat_slot = owner_rows * slot_count + slot_idx
-
-    upper = flat_slot >= slots // 2
-    slot_ids = jnp.arange(slots // 2, dtype=jnp.int32)
-    slot_key = jnp.where(upper, flat_slot - slots // 2, flat_slot)
-    pack = (slot_key[None, :] == slot_ids[:, None]).astype(BF16)
-    halves = jnp.concatenate(
-        [jnp.where(upper[:, None], 0.0, intensity), jnp.where(upper[:, None], intensity, 0.0)],
-        axis=1,
-    ).astype(BF16)
-    packed = jnp.dot(pack, halves, preferred_element_type=F32).astype(BF16)
-    send_values = jnp.concatenate([packed[:, :species], packed[:, species:]])
-    slot_hot = jnp.arange(slot_count, dtype=jnp.int32)[:, None] == slot_idx[None, :]
-    place_row = (land_cell // tile_width + 1).astype(F32)[None, :]
-    place_col = (land_cell % tile_width).astype(F32)[None, :]
-    places = jnp.concatenate(
-        [jnp.where(slot_hot, place_row, 0.0), jnp.where(slot_hot, place_col, 0.0)], axis=0
-    ).astype(BF16)
-    table = jnp.dot(places, owner_hot.astype(BF16), preferred_element_type=F32).astype(BF16).T
-    table = jnp.pad(table[:, None, :], ((0, 0), (0, 7), (0, species - 2 * slot_count)))
-    send = jnp.concatenate([send_values.reshape(devices, slot_count, species), table], axis=1)
+    send, flat_slot = pack(
+        owner.reshape(1, row_count),
+        land_cell.reshape(1, row_count),
+        intensity,
+        devices,
+        slot_count,
+        tile_width,
+    )
     got = lax.all_to_all(send, ALL, split_axis=0, concat_axis=0, tiled=True)
     send, own = lax.optimization_barrier((send, covariates))
     own_gates = gates(core[None], own, w_in, b_in)
@@ -523,7 +579,7 @@
     )
     home_values, density = lax.optimization_barrier((home_values, density))
     density = lax.all_to_all(density, ALL, 0, 0, tiled=True)
-    dlog = pick(flat_slot[None, :], home_values.reshape(slots, species), intensity)
+    dlog = pick(flat_slot, home_values.reshape(slots, species), intensity)
     peers = devices // 2
     pieces = backward(
         core[None],

time: 235 us -> 234 us (level)
  matrix products: 7.04 us -> 0 us
  local copies, waits for them, and re-layouts: 30.2 us -> 35.5 us
  other arithmetic: 7.19 us -> 4.04 us
  Pallas kernels: 69.8 us -> 72.9 us
    dot_general x3 -> x0, matrix products: 7.04 us -> none  [the longest x1 3.38 us: local(): jnp.dot(earlier, owner_hot.astype(BF16), preferred_element_type=F32)]
    unnamed x49 -> x55, local copies, waits for them, and re-layouts: 19.4 us -> 26 us
    pallas_call x0 -> x1, Pallas kernels: none -> 3.13 us  [pack(): pl.pallas_call(functools.partial(pack_body, wide), out_shape=[jax.ShapeDt...]
    concatenate x2 -> x0, other arithmetic: 2.56 us -> none  [the longest x1 1.29 us: local(): jnp.concatenate([send_values.reshape(devices, slot_count, species), table...]
where the time goes in v2:
time: 234 us; the launch traced here: 231 us
  Pallas kernels  72.9 us (31%)
  waiting for transfers between devices  54.2 us (23%)
  starting transfers between devices  39.8 us (17%)
  local copies, waits for them, and re-layouts  35.5 us (15%)
  blocking collectives  23.7 us (10%)
  other arithmetic  4.04 us (2%)
    all_to_all x1, waiting for transfers between devices, local(): pieces = lax.all_to_all(pieces, ('y', 'z', 'x'), 0, 0)  31.9 us
    unnamed x55, local copies, waits for them, and re-layouts  26 us
    all_to_all x1, blocking collectives, local(): lax.all_to_all(back_values.reshape(devices, slot_count, species), ALL, sp...  23.7 us
    pallas_call x1, Pallas kernels, backward(): pl.pallas_call(backward_body, out_shape=jax.ShapeDtypeStruct((peers, send...  16.5 us
    pallas_call x1, Pallas kernels, raster(): pl.pallas_call(functools.partial(raster_body, scale), out_shape=[jax.Shap...  15.4 us
    pallas_call x2, Pallas kernels, gates(): pl.pallas_call(gates_body, out_shape=[jax.ShapeDtypeStruct((rows, hid //...  14 us
    all_to_all x1, starting transfers between devices, local(): got = lax.all_to_all(send, ALL, split_axis=0, concat_axis=0, tiled=True)  11.6 us
    all_to_all x1, starting transfers between devices, local(): pieces = lax.all_to_all(pieces, ('y', 'z', 'x'), 0, 0)  10 us
  transfers between devices with their start and end apart: 8, of which 6 were waited for; matrix products, arithmetic and copies ran while one was open for 7% of the time, Pallas kernels for 18%

profile of v2, /device:TPU:0, one launch (start us, length us, event | category | flops | bytes accessed | tf_op | source)
XLA Modules:
  0.0 231.3 jit_solution(9032506600788791977)
XLA Ops:
  6.2 8.9 %land_forward.1.intensity_ref.refs_0_ = f32[2048,128]{1,0:T(8,128)S(1)} custom-call(bf16[2048,512]{1,0:T(8,128)(2,1)S(1)} %copy-done, bf16[512,2048]{1,0:T(8,128)(2,1)S(1)} %copy-done.2, f32[1,2048]{1,0:T(1,128)S(1)} %bitcast.49, bf16[2048,128]{1,0:T(8,128)(2,1)S(1)} %copy-done.10, f32[1,128]{1,0:T(1,128)S(1)} %bitcast.54), custom_call_target="tpu_custom_call" | custom-call | tf_op jit(solution)/shard_map/land_forward/pallas_call | solution.py:186
  15.1 3.1 %pack_cells.1 = (bf16[128,40,128]{2,1,0:T(8,128)(2,1)S(1)}, s32[1,2048]{1,0:T(1,128)S(1)}) custom-call(s32[1,2048]{1,0:T(1,128)S(1)} %bitcast.52, s32[1,2048]{1,0:T(1,128)S(1)} %bitcast.53, f32[2048,128]{1,0:T(8,128)S(1)} %land_forward.1.intensity_ref.refs_0_), custom_call_target="tpu_custom_call" | custom-call | tf_op jit(solution)/shard_map/pack_cells/pallas_call | solution.py:385
  19.3 11.6 %all-to-all-start = ((bf16[128,40,128]{2,1,0:T(8,128)(2,1)}), bf16[128,40,128]{2,1,0:T(8,128)(2,1)}, u32[]{:S(2)}, u32[]{:S(2)}) async-start(bf16[128,40,128]{2,1,0:T(8,128)(2,1)} %copy-done.13), calls=%async_computation | async-start | bytes 2621440 | tf_op jit(solution)/shard_map/all_to_all | solution.py:548
  31.3 2.4 %select_convert_fusion = bf16[16,128,128]{2,1,0:T(8,128)(2,1)} fusion(s32[16,128,128]{2,1,0:T(8,128)} %param.24, pred[16,128]{1,0:T(8,128)(4,1)S(1)} %broadcast_compare_fusion), kind=kLoop, calls=%fused_computation.1 | loop fusion | flops 524288 | bytes 1574912 | tf_op jit(solution)/shard_map/convert_element_type | solution.py:556
  33.6 2.0 copy.48
  39.2 6.3 %land_gates.2 = (bf16[2048,1024]{1,0:T(8,128)(2,1)S(1)}, f32[2048,1024]{1,0:T(8,128)}) custom-call(s32[1]{0:T(128)} %bitcast.core_ref, bf16[2048,512]{1,0:T(8,128)(2,1)S(1)} %copy-done.1, bf16[512,2048]{1,0:T(8,128)(2,1)S(1)} %copy-done.3, f32[1,2048]{1,0:T(1,128)S(1)} %bitcast.50), custom_call_target="tpu_custom_call" | custom-call | tf_op jit(solution)/shard_map/land_gates/pallas_call | solution.py:217
  47.4 4.9 %all-to-all-done.got_ref = bf16[128,40,128]{2,1,0:T(8,128)(2,1)} async-done(((bf16[128,40,128]{2,1,0:T(8,128)(2,1)}), bf16[128,40,128]{2,1,0:T(8,128)(2,1)}, u32[]{:S(2)}, u32[]{:S(2)}) %all-to-all-start) | async-done | bytes 1310752 | tf_op jit(solution)/shard_map/all_to_all | solution.py:548
  53.4 6.7 %place_cells.1 = bf16[128,32,128]{2,1,0:T(8,128)(2,1)S(1)} custom-call(bf16[128,40,128]{2,1,0:T(8,128)(2,1)} %all-to-all-done.got_ref, bf16[128,16,128]{2,1,0:T(8,128)(2,1)S(1)} %bitcast.48), custom_call_target="tpu_custom_call" | custom-call | tf_op jit(solution)/shard_map/place_cells/pallas_call | solution.py:450
  61.0 6.0 %all-to-all-start.1 = ((bf16[128,32,128]{2,1,0:T(8,128)(2,1)}), bf16[128,32,128]{2,1,0:T(8,128)(2,1)}, u32[]{:S(2)}, u32[]{:S(2)}) async-start(bf16[128,32,128]{2,1,0:T(8,128)(2,1)} %copy-done.9), calls=%async_computation.1 | async-start | bytes 2097152 | tf_op jit(solution)/shard_map/all_to_all | solution.py:565
  68.9 7.8 %land_gates.3 = (bf16[2048,1024]{1,0:T(8,128)(2,1)S(1)}, f32[2048,1024]{1,0:T(8,128)}) custom-call(s32[1]{0:T(128)} %bitcast.core_ref, bf16[2048,512]{1,0:T(8,128)(2,1)} %collective-permute-done.x_ref.x_other, bf16[512,2048]{1,0:T(8,128)(2,1)S(1)} %copy-done.4, f32[1,2048]{1,0:T(1,128)S(1)} %bitcast.51), custom_call_target="tpu_custom_call" | custom-call | tf_op jit(solution)/shard_map/land_gates/pallas_call | solution.py:217
  78.7 6.8 %all-to-all-done.1.got_ref = bf16[128,32,128]{2,1,0:T(8,128)(2,1)} async-done(((bf16[128,32,128]{2,1,0:T(8,128)(2,1)}), bf16[128,32,128]{2,1,0:T(8,128)(2,1)}, u32[]{:S(2)}, u32[]{:S(2)}) %all-to-all-start.1) | async-done | bytes 1048608 | tf_op jit(solution)/shard_map/all_to_all | solution.py:565
  85.4 15.4 %raster_steps.1 = (f32[128,16,128]{2,1,0:T(8,128)S(1)}, bf16[128,16,128]{2,1,0:T(8,128)(2,1)S(1)}) custom-call(f32[1,32]{1,0:T(1,128)S(1)} %pad_dynamic-slice_fusion.species_ref, bf16[128,32,128]{2,1,0:T(8,128)(2,1)} %all-to-all-done.1.got_ref), custom_call_target="tpu_custom_call" | custom-call | tf_op jit(solution)/shard_map/raster_steps/pallas_call | solution.py:147
  102.5 5.7 %all-to-all-start.2 = ((bf16[128,16,128]{2,1,0:T(8,128)(2,1)}), bf16[128,16,128]{2,1,0:T(8,128)(2,1)}, u32[]{:S(2)}, u32[]{:S(2)}) async-start(bf16[128,16,128]{2,1,0:T(8,128)(2,1)} %copy-done.15), calls=%async_computation.2 | async-start | bytes 1048576 | tf_op jit(solution)/shard_map/all_to_all | solution.py:570
  109.7 3.5 %reshape.100.index_ref = s32[4096,1]{1,0:T(8,128)} reshape(s32[128,32]{1,0:T(8,128)S(1)} %fusion) | data formatting | bytes 32768 | tf_op jit(solution)/shard_map/jit(_where)/select_n | solution.py:554
  113.3 8.2 %all-to-all-done.2 = bf16[128,16,128]{2,1,0:T(8,128)(2,1)} async-done(((bf16[128,16,128]{2,1,0:T(8,128)(2,1)}), bf16[128,16,128]{2,1,0:T(8,128)(2,1)}, u32[]{:S(2)}, u32[]{:S(2)}) %all-to-all-start.2) | async-done | bytes 524320 | tf_op jit(solution)/shard_map/all_to_all | solution.py:570
  124.2 4.5 %pick_rows.2 = bf16[4096,128]{1,0:T(8,128)(2,1)S(1)} custom-call(s32[4096,1]{1,0:T(8,128)S(1)} %copy-done.5, bf16[128,2048]{1,0:T(8,128)(2,1)S(1)} %bitcast.47), custom_call_target="tpu_custom_call" | custom-call | tf_op jit(solution)/shard_map/pick_rows/pallas_call | solution.py:492
  128.7 23.7 %all_to_all.30 = bf16[128,32,128]{2,1,0:T(8,128)(2,1)} all-to-all(bf16[128,32,128]{2,1,0:T(8,128)(2,1)S(1)} %bitcast.45), channel_id=1, replica_groups=mesh['y'=4,'core'=2,'z'=4,'x'=4] {'y','core','z','x'}, dimensions={0} | all-to-all | bytes 2097152 | tf_op jit(solution)/shard_map/all_to_all | solution.py:573
  152.4 5.8 %all-to-all-start.4 = ((f32[128,16,128]{2,1,0:T(8,128)}), f32[128,16,128]{2,1,0:T(8,128)}, u32[]{:S(2)}, u32[]{:S(2)}) async-start(f32[128,16,128]{2,1,0:T(8,128)} %copy-done.14), calls=%async_computation.4 | async-start | bytes 2097152 | tf_op jit(solution)/shard_map/all_to_all | solution.py:581
  159.4 3.9 %pick_rows.3.dlog_own = bf16[2048,128]{1,0:T(8,128)(2,1)S(1)} custom-call(s32[1,2048]{1,0:T(1,128)S(1)} %get-tuple-element.31.index_ref, bf16[4096,128]{1,0:T(8,128)(2,1)S(1)} %bitcast.46, f32[2048,128]{1,0:T(8,128)S(1)} %land_forward.1.intensity_ref.refs_0_), custom_call_target="tpu_custom_call" | custom-call | tf_op jit(solution)/shard_map/pick_rows/pallas_call | solution.py:492
  165.6 16.5 %land_backward.1 = f32[64,80,128]{2,1,0:T(8,128)} custom-call(s32[1]{0:T(128)} %bitcast.core_ref, bf16[2048,512]{1,0:T(8,128)(2,1)S(1)} %copy-done.1, bf16[2048,512]{1,0:T(8,128)(2,1)} %collective-permute-done.x_ref.x_other, bf16[2048,128]{1,0:T(8,128)(2,1)S(1)} %pick_rows.3.dlog_own, bf16[2048,128]{1,0:T(8,128)(2,1)S(1)} %collective-permute-done.1.dlog_other, ...), custom_call_target="tpu_custom_call" | custom-call | tf_op jit(solution)/shard_map/land_backward/pallas_call | solution.py:314
  182.1 10.0 %all-to-all-start.5 = ((f32[64,80,128]{2,1,0:T(8,128)}), f32[64,80,128]{2,1,0:T(8,128)S(1)}, u32[]{:S(2)}, u32[]{:S(2)}) async-start(f32[64,80,128]{2,1,0:T(8,128)} %land_backward.1), calls=%async_computation.5 | async-start | bytes 5242880 | tf_op jit(solution)/shard_map/all_to_all | solution.py:595
  192.2 2.5 %copy.62 = f32[16,8,16,128]{3,1,2,0:T(8,128)} copy(f32[16,8,16,128]{3,2,1,0:T(8,128)} %bitcast.27) | data formatting | bytes 2097152
  194.7 2.5 %copy.51 = f32[2048,128]{1,0:T(8,128)} copy(f32[2048,128]{0,1:T(8,128)} %bitcast.55) | data formatting | bytes 2097152 | tf_op jit(solution)/shard_map/transpose | solution.py:594
  197.2 31.9 %all-to-all-done.5 = f32[64,80,128]{2,1,0:T(8,128)S(1)} async-done(((f32[64,80,128]{2,1,0:T(8,128)}), f32[64,80,128]{2,1,0:T(8,128)S(1)}, u32[]{:S(2)}, u32[]{:S(2)}) %all-to-all-start.5) | async-done | bytes 2621472 | tf_op jit(solution)/shard_map/all_to_all | solution.py:595
  (77 shorter events, 29.7 us)
Async XLA Ops:
  0.6 1.6 copy-start
  6.2 8.9 %copy-start.18 = (s32[2048,1]{0,1:T(1,128)S(1)}, s32[2048,1]{0,1:T(1,128)}, u32[]{:S(2)}) copy-start(s32[2048,1]{0,1:T(1,128)} %param.18) | copy-start | bytes 24580
  6.2 8.9 %copy-start.19 = (s32[2048]{0:T(1024)S(1)}, s32[2048]{0:T(1024)}, u32[]{:S(2)}) copy-start(s32[2048]{0:T(1024)} %param.19) | copy-start | bytes 24580
  15.1 15.9 %copy-start.1 = (bf16[2048,512]{1,0:T(8,128)(2,1)S(1)}, bf16[2048,512]{1,0:T(8,128)(2,1)}, u32[]{:S(2)}) copy-start(bf16[2048,512]{1,0:T(8,128)(2,1)} %x_own.1) | copy-start | bytes 6291460
  15.1 16.1 %copy-start.23 = (s32[16,128]{1,0:T(8,128)S(1)}, s32[16,128]{1,0:T(8,128)}, u32[]{:S(2)}) copy-start(s32[16,128]{1,0:T(8,128)} %param.25) | copy-start | bytes 24580
  19.3 33.0 %all-to-all-start = ((bf16[128,40,128]{2,1,0:T(8,128)(2,1)}), bf16[128,40,128]{2,1,0:T(8,128)(2,1)}, u32[]{:S(2)}, u32[]{:S(2)}) async-start(bf16[128,40,128]{2,1,0:T(8,128)(2,1)} %copy-done.13), calls=%async_computation | async-start | bytes 2621440 | tf_op jit(solution)/shard_map/all_to_all | solution.py:548
  30.9 6.7 %copy-start.17 = (f32[2048]{0:T(1024)S(1)}, f32[2048]{0:T(1024)}, u32[]{:S(2)}) copy-start(f32[2048]{0:T(1024)} %param.15) | copy-start | bytes 24580
  31.0 36.3 %collective-permute-start = (bf16[2048,512]{1,0:T(8,128)(2,1)S(1)}, bf16[2048,512]{1,0:T(8,128)(2,1)}, u32[]{:S(2)}, u32[]{:S(2)}) collective-permute-start(bf16[2048,512]{1,0:T(8,128)(2,1)S(1)} %copy-done.1), channel_id=1, source_target_pairs={{0,16},{16,0},{1,17},{17,1},{2,18},{18,2},{3,19},{19,3},{4,20},{20... | collective-permute-start | bytes 6291464 | tf_op jit(solution)/shard_map/ppermute | solution.py:510
  37.6 1.6 copy-start.3
  45.5 2.0 copy-start.6
  53.4 13.7 %copy-start.22 = (f32[128,9]{0,1:T(8,128)S(1)}, f32[128,9]{0,1:T(8,128)}, u32[]{:S(2)}) copy-start(f32[128,9]{0,1:T(8,128)} %param.20) | copy-start | bytes 13828
  53.4 13.7 %copy-start.21 = (f32[128,9]{0,1:T(8,128)S(1)}, f32[128,9]{0,1:T(8,128)}, u32[]{:S(2)}) copy-start(f32[128,9]{0,1:T(8,128)} %param.21) | copy-start | bytes 13828
  53.4 13.7 %copy-start.24 = (f32[128]{0:T(128)S(1)}, f32[128]{0:T(128)}, u32[]{:S(2)}) copy-start(f32[128]{0:T(128)} %param.23) | copy-start | bytes 1540
  53.4 13.7 %copy-start.25 = (f32[128]{0:T(128)S(1)}, f32[128]{0:T(128)}, u32[]{:S(2)}) copy-start(f32[128]{0:T(128)} %param.22) | copy-start | bytes 1540
  61.0 24.4 %all-to-all-start.1 = ((bf16[128,32,128]{2,1,0:T(8,128)(2,1)}), bf16[128,32,128]{2,1,0:T(8,128)(2,1)}, u32[]{:S(2)}, u32[]{:S(2)}) async-start(bf16[128,32,128]{2,1,0:T(8,128)(2,1)} %copy-done.9), calls=%async_computation.1 | async-start | bytes 2097152 | tf_op jit(solution)/shard_map/all_to_all | solution.py:565
  67.3 1.6 copy-start.4
  76.6 2.0 copy-start.7
  102.5 18.9 %all-to-all-start.2 = ((bf16[128,16,128]{2,1,0:T(8,128)(2,1)}), bf16[128,16,128]{2,1,0:T(8,128)(2,1)}, u32[]{:S(2)}, u32[]{:S(2)}) async-start(bf16[128,16,128]{2,1,0:T(8,128)(2,1)} %copy-done.15), calls=%async_computation.2 | async-start | bytes 1048576 | tf_op jit(solution)/shard_map/all_to_all | solution.py:570
  122.7 1.6 copy-start.5
  152.4 29.7 %all-to-all-start.4 = ((f32[128,16,128]{2,1,0:T(8,128)}), f32[128,16,128]{2,1,0:T(8,128)}, u32[]{:S(2)}, u32[]{:S(2)}) async-start(f32[128,16,128]{2,1,0:T(8,128)} %copy-done.14), calls=%async_computation.4 | async-start | bytes 2097152 | tf_op jit(solution)/shard_map/all_to_all | solution.py:581
  159.4 6.2 %copy-start.11 = (bf16[2048,128]{1,0:T(8,128)(2,1)S(1)}, bf16[2048,128]{1,0:T(8,128)(2,1)}, u32[]{:S(2)}) copy-start(bf16[2048,128]{1,0:T(8,128)(2,1)} %w_out_ref.3) | copy-start | bytes 1572868
  163.4 2.3 collective-permute-start.1
  182.1 47.0 %all-to-all-start.5 = ((f32[64,80,128]{2,1,0:T(8,128)}), f32[64,80,128]{2,1,0:T(8,128)S(1)}, u32[]{:S(2)}, u32[]{:S(2)}) async-start(f32[64,80,128]{2,1,0:T(8,128)} %land_backward.1), calls=%async_computation.5 | async-start | bytes 5242880 | tf_op jit(solution)/shard_map/all_to_all | solution.py:595
  229.3 1.3 collective-permute-start.2
  (10 other events, 10.0 us)

commit v3 on v2

--- a/solution.py
+++ b/solution.py
@@ -147,8 +147,8 @@
     return pl.pallas_call(
         functools.partial(raster_body, scale),
         out_shape=[
-            jax.ShapeDtypeStruct((tiles, tall, lanes), F32),
-            jax.ShapeDtypeStruct((tiles, tall, lanes), BF16),
+            pltpu.HBM((tiles, tall, lanes), F32),
+            pltpu.HBM((tiles, tall, lanes), BF16),
         ],
         in_specs=[pl.BlockSpec(memory_space=pltpu.SMEM), whole(got.shape)],
         out_specs=[whole((tiles, tall, lanes))] * 2,
@@ -197,7 +197,7 @@
         out_specs=pl.BlockSpec((block, species), lambda i: (i, 0)),
         compiler_params=pltpu.CompilerParams(vmem_limit_bytes=40 << 20),
         name="land_forward",
-    )(x, w_in, b_in[None, :], w_out, b_out[None, :])
+    )(*in_hbm(x, w_in), b_in[None, :], *in_hbm(w_out), b_out[None, :])
 
 
 def gates_body(core_ref, x_ref, w_in_ref, b_in_ref, hidden_ref, slope_ref):
@@ -217,8 +217,8 @@
     return pl.pallas_call(
         gates_body,
         out_shape=[
-            jax.ShapeDtypeStruct((rows, hid // 2), BF16),
-            jax.ShapeDtypeStruct((rows, hid // 2), F32),
+            pltpu.HBM((rows, hid // 2), BF16),
+            pltpu.HBM((rows, hid // 2), F32),
         ],
         grid_spec=pltpu.PrefetchScalarGridSpec(
             num_scalar_prefetch=1,
@@ -232,7 +232,7 @@
         ),
         compiler_params=pltpu.CompilerParams(vmem_limit_bytes=40 << 20),
         name="land_gates",
-    )(core, x, w_in, b_in[None, :])
+    )(core, *in_hbm(x, w_in), b_in[None, :])
 
 
 def backward_body(
@@ -320,6 +320,10 @@
     )(core, *x, *dlog, *hidden, *slope, w_out)
 
 
+def in_hbm(*arrays):
+    return tuple(pltpu.with_memory_space_constraint(array, pltpu.HBM) for array in arrays)
+
+
 def pack_body(wide, owner_ref, cell_ref, intensity_ref, send_ref, slot_ref):
     devices, tall, species = send_ref.shape
     slot_count = tall - 8
@@ -385,7 +389,7 @@
     return pl.pallas_call(
         functools.partial(pack_body, wide),
         out_shape=[
-            jax.ShapeDtypeStruct((devices, slot_count + 8, species), BF16),
+            pltpu.HBM((devices, slot_count + 8, species), BF16),
             jax.ShapeDtypeStruct((1, rows), jnp.int32),
         ],
         in_specs=[whole((1, rows)), whole((1, rows)), whole((rows, species))],
@@ -449,13 +453,13 @@
 
     return pl.pallas_call(
         functools.partial(place_body, slot_count),
-        out_shape=jax.ShapeDtypeStruct((species, 2 * tall, wide), BF16),
+        out_shape=pltpu.HBM((species, 2 * tall, wide), BF16),
         in_specs=[whole(got.shape), whole(code.shape)],
         out_specs=whole((species, 2 * tall, wide)),
         scratch_shapes=[pltpu.VMEM((tall * wide // 2, 2 * species), F32)],
         compiler_params=pltpu.CompilerParams(vmem_limit_bytes=40 << 20),
         name="place_cells",
-    )(got, code)
+    )(*in_hbm(got, code))
 
 
 def pick_body(wide, index_ref, table_ref, *refs):
@@ -503,7 +507,7 @@
         out_specs=block_spec,
         compiler_params=pltpu.CompilerParams(vmem_limit_bytes=40 << 20),
         name="pick_rows",
-    )(index, table, *more)
+    )(*in_hbm(index, table), *more)
 
 
 def other_core(values):

time: 234 us -> 232 us (level)
  local copies, waits for them, and re-layouts: 35.5 us -> 14.7 us
  Pallas kernels: 72.9 us -> 84 us
  waiting for transfers between devices: 54.2 us -> 61.4 us
    unnamed x55 -> x31, local copies, waits for them, and re-layouts: 26 us -> 6.45 us
    pallas_call x5, Pallas kernels: 39.2 us -> 44.6 us  [the longest x2 16.5 us: gates(): pl.pallas_call(gates_body, out_shape=[pltpu.HBM((rows, hid // 2), BF16),...]
    pallas_call x2, Pallas kernels: 8.38 us -> 12.1 us  [pick(): pl.pallas_call(functools.partial(pick_body, wide), out_shape=jax.ShapeDty...]
    all_to_all x1, waiting for transfers between devices: 6.75 us -> 9.89 us  [local(): got = lax.all_to_all(send, ALL, 0, 0, tiled=True)]
  transfers between devices with their start and end apart: 8 -> 8, of which waited for: 6 -> 6; matrix products, arithmetic and copies ran while one was open for 7% -> 7% of each run, Pallas kernels for 18% -> 20%
where the time goes in v3:
time: 232 us; the launch traced here: 230 us
  Pallas kernels  84 us (36%)
  waiting for transfers between devices  61.4 us (26%)
  starting transfers between devices  39.1 us (17%)
  blocking collectives  23.7 us (10%)
  local copies, waits for them, and re-layouts  14.7 us (6%)
  other arithmetic  5.79 us (2%)
    all_to_all x1, waiting for transfers between devices, local(): pieces = lax.all_to_all(pieces, ('y', 'z', 'x'), 0, 0)  33.9 us
    all_to_all x1, blocking collectives, local(): lax.all_to_all(back_values.reshape(devices, slot_count, species), ALL, sp...  23.7 us
    pallas_call x1, Pallas kernels, backward(): pl.pallas_call(backward_body, out_shape=jax.ShapeDtypeStruct((peers, send...  16.5 us
    pallas_call x2, Pallas kernels, gates(): pl.pallas_call(gates_body, out_shape=[pltpu.HBM((rows, hid // 2), BF16),...  16.5 us
    pallas_call x1, Pallas kernels, raster(): pl.pallas_call(functools.partial(raster_body, scale), out_shape=[pltpu.HB...  16.2 us
    pallas_call x2, Pallas kernels, pick(): pl.pallas_call(functools.partial(pick_body, wide), out_shape=jax.ShapeDty...  12.1 us
    all_to_all x1, starting transfers between devices, local(): got = lax.all_to_all(send, ALL, split_axis=0, concat_axis=0, tiled=True)  11.6 us
    pallas_call x1, Pallas kernels, forward(): pl.pallas_call(forward_body, out_shape=jax.ShapeDtypeStruct((rows, specie...  10.8 us
  transfers between devices with their start and end apart: 8, of which 6 were waited for; matrix products, arithmetic and copies ran while one was open for 7% of the time, Pallas kernels for 20%

profile of v3, /device:TPU:0, one launch (start us, length us, event | category | flops | bytes accessed | tf_op | source)
XLA Modules:
  0.0 229.6 jit_solution(3225303673550202934)
XLA Ops:
  2.0 10.8 %land_forward.1.intensity_ref.refs_0_ = f32[2048,128]{1,0:T(8,128)S(1)} custom-call(bf16[2048,512]{1,0:T(8,128)(2,1)} %x_own.1, bf16[512,2048]{1,0:T(8,128)(2,1)} %w_in_ref.5, f32[1,2048]{1,0:T(1,128)S(1)} %bitcast.46, bf16[2048,128]{1,0:T(8,128)(2,1)} %w_out_ref.3, f32[1,128]{1,0:T(1,128)S(1)} %bitcast.51), custom_call_target="tpu_custom_call" | custom-call | tf_op jit(solution)/shard_map/land_forward/pallas_call | solution.py:186
  12.8 4.2 %pack_cells.1 = (bf16[128,40,128]{2,1,0:T(8,128)(2,1)}, s32[1,2048]{1,0:T(1,128)S(1)}) custom-call(s32[1,2048]{1,0:T(1,128)S(1)} %bitcast.49, s32[1,2048]{1,0:T(1,128)S(1)} %bitcast.50, f32[2048,128]{1,0:T(8,128)S(1)} %land_forward.1.intensity_ref.refs_0_), custom_call_target="tpu_custom_call" | custom-call | tf_op jit(solution)/shard_map/pack_cells/pallas_call | solution.py:389
  17.6 11.6 %all-to-all-start = ((bf16[128,40,128]{2,1,0:T(8,128)(2,1)}), bf16[128,40,128]{2,1,0:T(8,128)(2,1)}, u32[]{:S(2)}, u32[]{:S(2)}) async-start(bf16[128,40,128]{2,1,0:T(8,128)(2,1)} %get-tuple-element.25), calls=%async_computation | async-start | bytes 2621440 | tf_op jit(solution)/shard_map/all_to_all | solution.py:552
  29.5 2.4 %select_convert_fusion = bf16[16,128,128]{2,1,0:T(8,128)(2,1)} fusion(s32[16,128,128]{2,1,0:T(8,128)} %param.24, pred[16,128]{1,0:T(8,128)(4,1)S(1)} %broadcast_compare_fusion), kind=kLoop, calls=%fused_computation.1 | loop fusion | flops 524288 | bytes 1574912 | tf_op jit(solution)/shard_map/convert_element_type | solution.py:560
  31.9 2.0 copy.48
  33.9 2.0 copy.57
  35.9 8.3 %land_gates.2 = (bf16[2048,1024]{1,0:T(8,128)(2,1)}, f32[2048,1024]{1,0:T(8,128)}) custom-call(s32[1]{0:T(128)} %bitcast.core_ref, bf16[2048,512]{1,0:T(8,128)(2,1)} %x_own.1, bf16[512,2048]{1,0:T(8,128)(2,1)} %w_in_ref.5, f32[1,2048]{1,0:T(1,128)S(1)} %bitcast.47), custom_call_target="tpu_custom_call" | custom-call | tf_op jit(solution)/shard_map/land_gates/pallas_call | solution.py:217
  44.1 6.5 %all-to-all-done.got_ref = bf16[128,40,128]{2,1,0:T(8,128)(2,1)} async-done(((bf16[128,40,128]{2,1,0:T(8,128)(2,1)}), bf16[128,40,128]{2,1,0:T(8,128)(2,1)}, u32[]{:S(2)}, u32[]{:S(2)}) %all-to-all-start) | async-done | bytes 1310752 | tf_op jit(solution)/shard_map/all_to_all | solution.py:552
  50.6 7.7 %place_cells.1 = bf16[128,32,128]{2,1,0:T(8,128)(2,1)} custom-call(bf16[128,40,128]{2,1,0:T(8,128)(2,1)} %all-to-all-done.got_ref, bf16[128,16,128]{2,1,0:T(8,128)(2,1)} %bitcast.58), custom_call_target="tpu_custom_call" | custom-call | tf_op jit(solution)/shard_map/place_cells/pallas_call | solution.py:454
  58.4 6.0 %all-to-all-start.1 = ((bf16[128,32,128]{2,1,0:T(8,128)(2,1)}), bf16[128,32,128]{2,1,0:T(8,128)(2,1)}, u32[]{:S(2)}, u32[]{:S(2)}) async-start(bf16[128,32,128]{2,1,0:T(8,128)(2,1)} %place_cells.1), calls=%async_computation.1 | async-start | bytes 2097152 | tf_op jit(solution)/shard_map/all_to_all | solution.py:569
  64.6 8.3 %land_gates.3 = (bf16[2048,1024]{1,0:T(8,128)(2,1)}, f32[2048,1024]{1,0:T(8,128)}) custom-call(s32[1]{0:T(128)} %bitcast.core_ref, bf16[2048,512]{1,0:T(8,128)(2,1)} %collective-permute-done.x_ref.x_other, bf16[512,2048]{1,0:T(8,128)(2,1)} %w_in_ref.5, f32[1,2048]{1,0:T(1,128)S(1)} %bitcast.48), custom_call_target="tpu_custom_call" | custom-call | tf_op jit(solution)/shard_map/land_gates/pallas_call | solution.py:217
  72.9 9.9 %all-to-all-done.1.got_ref = bf16[128,32,128]{2,1,0:T(8,128)(2,1)} async-done(((bf16[128,32,128]{2,1,0:T(8,128)(2,1)}), bf16[128,32,128]{2,1,0:T(8,128)(2,1)}, u32[]{:S(2)}, u32[]{:S(2)}) %all-to-all-start.1) | async-done | bytes 1048608 | tf_op jit(solution)/shard_map/all_to_all | solution.py:569
  82.7 16.2 %raster_steps.1 = (f32[128,16,128]{2,1,0:T(8,128)}, bf16[128,16,128]{2,1,0:T(8,128)(2,1)}) custom-call(f32[1,32]{1,0:T(1,128)S(1)} %pad_dynamic-slice_fusion.species_ref, bf16[128,32,128]{2,1,0:T(8,128)(2,1)} %all-to-all-done.1.got_ref), custom_call_target="tpu_custom_call" | custom-call | tf_op jit(solution)/shard_map/raster_steps/pallas_call | solution.py:147
  98.9 4.6 %all-to-all-start.2 = ((bf16[128,16,128]{2,1,0:T(8,128)(2,1)}), bf16[128,16,128]{2,1,0:T(8,128)(2,1)S(1)}, u32[]{:S(2)}, u32[]{:S(2)}) async-start(bf16[128,16,128]{2,1,0:T(8,128)(2,1)} %get-tuple-element.35), calls=%async_computation.2 | async-start | bytes 1048576 | tf_op jit(solution)/shard_map/all_to_all | solution.py:574
  105.0 3.6 %reshape.100.index_ref = s32[4096,1]{1,0:T(8,128)} reshape(s32[128,32]{1,0:T(8,128)S(1)} %fusion) | data formatting | bytes 32768 | tf_op jit(solution)/shard_map/jit(_where)/select_n | solution.py:558
  108.5 8.6 %all-to-all-done.2 = bf16[128,16,128]{2,1,0:T(8,128)(2,1)S(1)} async-done(((bf16[128,16,128]{2,1,0:T(8,128)(2,1)}), bf16[128,16,128]{2,1,0:T(8,128)(2,1)S(1)}, u32[]{:S(2)}, u32[]{:S(2)}) %all-to-all-start.2) | async-done | bytes 524320 | tf_op jit(solution)/shard_map/all_to_all | solution.py:574
  118.1 6.8 %pick_rows.2 = bf16[4096,128]{1,0:T(8,128)(2,1)S(1)} custom-call(s32[4096,1]{1,0:T(8,128)} %reshape.100.index_ref, bf16[128,2048]{1,0:T(8,128)(2,1)} %bitcast.54), custom_call_target="tpu_custom_call" | custom-call | tf_op jit(solution)/shard_map/pick_rows/pallas_call | solution.py:496
  124.9 23.7 %all_to_all.30 = bf16[128,32,128]{2,1,0:T(8,128)(2,1)} all-to-all(bf16[128,32,128]{2,1,0:T(8,128)(2,1)S(1)} %bitcast.45), channel_id=1, replica_groups=mesh['y'=4,'core'=2,'z'=4,'x'=4] {'y','core','z','x'}, dimensions={0} | all-to-all | bytes 2097152 | tf_op jit(solution)/shard_map/all_to_all | solution.py:577
  148.6 5.9 %all-to-all-start.4 = ((f32[128,16,128]{2,1,0:T(8,128)}), f32[128,16,128]{2,1,0:T(8,128)}, u32[]{:S(2)}, u32[]{:S(2)}) async-start(f32[128,16,128]{2,1,0:T(8,128)} %get-tuple-element.42), calls=%async_computation.4 | async-start | bytes 2097152 | tf_op jit(solution)/shard_map/all_to_all | solution.py:585
  154.6 5.3 %pick_rows.3.dlog_own = bf16[2048,128]{1,0:T(8,128)(2,1)S(1)} custom-call(s32[1,2048]{1,0:T(1,128)} %copy-done.7, bf16[4096,128]{1,0:T(8,128)(2,1)} %bitcast.52, f32[2048,128]{1,0:T(8,128)S(1)} %land_forward.1.intensity_ref.refs_0_), custom_call_target="tpu_custom_call" | custom-call | tf_op jit(solution)/shard_map/pick_rows/pallas_call | solution.py:496
  162.1 16.5 %land_backward.1 = f32[64,80,128]{2,1,0:T(8,128)} custom-call(s32[1]{0:T(128)} %bitcast.core_ref, bf16[2048,512]{1,0:T(8,128)(2,1)S(1)} %copy-done.1, bf16[2048,512]{1,0:T(8,128)(2,1)} %collective-permute-done.x_ref.x_other, bf16[2048,128]{1,0:T(8,128)(2,1)S(1)} %pick_rows.3.dlog_own, bf16[2048,128]{1,0:T(8,128)(2,1)S(1)} %collective-permute-done.1.dlog_other, ...), custom_call_target="tpu_custom_call" | custom-call | tf_op jit(solution)/shard_map/land_backward/pallas_call | solution.py:314
  178.6 10.3 %all-to-all-start.5 = ((f32[64,80,128]{2,1,0:T(8,128)}), f32[64,80,128]{2,1,0:T(8,128)}, u32[]{:S(2)}, u32[]{:S(2)}) async-start(f32[64,80,128]{2,1,0:T(8,128)} %land_backward.1), calls=%async_computation.5 | async-start | bytes 5242880 | tf_op jit(solution)/shard_map/all_to_all | solution.py:599
  191.8 33.9 %all-to-all-done.5 = f32[64,80,128]{2,1,0:T(8,128)} async-done(((f32[64,80,128]{2,1,0:T(8,128)}), f32[64,80,128]{2,1,0:T(8,128)}, u32[]{:S(2)}, u32[]{:S(2)}) %all-to-all-start.5) | async-done | bytes 2621472 | tf_op jit(solution)/shard_map/all_to_all | solution.py:599
  225.7 1.9 reduce_sum.29
  (53 shorter events, 11.9 us)
Async XLA Ops:
  0.6 0.7 copy-start.3
  1.3 0.7 copy-start.8
  2.0 10.8 %copy-start.5 = (s32[2048,1]{0,1:T(1,128)S(1)}, s32[2048,1]{0,1:T(1,128)}, u32[]{:S(2)}) copy-start(s32[2048,1]{0,1:T(1,128)} %param.18) | copy-start | bytes 24580
  2.0 10.8 %copy-start.6 = (s32[2048]{0:T(1024)S(1)}, s32[2048]{0:T(1024)}, u32[]{:S(2)}) copy-start(s32[2048]{0:T(1024)} %param.19) | copy-start | bytes 24580
  12.8 16.5 %copy-start = (bf16[2048,512]{1,0:T(8,128)(2,1)S(1)}, bf16[2048,512]{1,0:T(8,128)(2,1)}, u32[]{:S(2)}) copy-start(bf16[2048,512]{1,0:T(8,128)(2,1)} %x_own.1) | copy-start | bytes 6291460
  12.8 16.8 %copy-start.11 = (s32[16,128]{1,0:T(8,128)S(1)}, s32[16,128]{1,0:T(8,128)}, u32[]{:S(2)}) copy-start(s32[16,128]{1,0:T(8,128)} %param.25) | copy-start | bytes 24580
  17.0 0.6 copy-start.7
  17.6 33.0 %all-to-all-start = ((bf16[128,40,128]{2,1,0:T(8,128)(2,1)}), bf16[128,40,128]{2,1,0:T(8,128)(2,1)}, u32[]{:S(2)}, u32[]{:S(2)}) async-start(bf16[128,40,128]{2,1,0:T(8,128)(2,1)} %get-tuple-element.25), calls=%async_computation | async-start | bytes 2621440 | tf_op jit(solution)/shard_map/all_to_all | solution.py:552
  29.2 6.7 %copy-start.4 = (f32[2048]{0:T(1024)S(1)}, f32[2048]{0:T(1024)}, u32[]{:S(2)}) copy-start(f32[2048]{0:T(1024)} %param.15) | copy-start | bytes 24580
  29.2 35.4 %collective-permute-start = (bf16[2048,512]{1,0:T(8,128)(2,1)S(1)}, bf16[2048,512]{1,0:T(8,128)(2,1)}, u32[]{:S(2)}, u32[]{:S(2)}) collective-permute-start(bf16[2048,512]{1,0:T(8,128)(2,1)S(1)} %copy-done), channel_id=1, source_target_pairs={{0,16},{16,0},{1,17},{17,1},{2,18},{18,2},{3,19},{19,3},{4,20},{20... | collective-permute-start | bytes 6291464 | tf_op jit(solution)/shard_map/ppermute | solution.py:514
  50.6 13.7 %copy-start.10 = (f32[128,9]{0,1:T(8,128)S(1)}, f32[128,9]{0,1:T(8,128)}, u32[]{:S(2)}) copy-start(f32[128,9]{0,1:T(8,128)} %param.20) | copy-start | bytes 13828
  50.6 13.8 %copy-start.9 = (f32[128,9]{0,1:T(8,128)S(1)}, f32[128,9]{0,1:T(8,128)}, u32[]{:S(2)}) copy-start(f32[128,9]{0,1:T(8,128)} %param.21) | copy-start | bytes 13828
  50.6 13.8 %copy-start.12 = (f32[128]{0:T(128)S(1)}, f32[128]{0:T(128)}, u32[]{:S(2)}) copy-start(f32[128]{0:T(128)} %param.23) | copy-start | bytes 1540
  50.6 13.8 %copy-start.13 = (f32[128]{0:T(128)S(1)}, f32[128]{0:T(128)}, u32[]{:S(2)}) copy-start(f32[128]{0:T(128)} %param.22) | copy-start | bytes 1540
  58.4 24.4 %all-to-all-start.1 = ((bf16[128,32,128]{2,1,0:T(8,128)(2,1)}), bf16[128,32,128]{2,1,0:T(8,128)(2,1)}, u32[]{:S(2)}, u32[]{:S(2)}) async-start(bf16[128,32,128]{2,1,0:T(8,128)(2,1)} %place_cells.1), calls=%async_computation.1 | async-start | bytes 2097152 | tf_op jit(solution)/shard_map/all_to_all | solution.py:569
  98.9 18.2 %all-to-all-start.2 = ((bf16[128,16,128]{2,1,0:T(8,128)(2,1)}), bf16[128,16,128]{2,1,0:T(8,128)(2,1)S(1)}, u32[]{:S(2)}, u32[]{:S(2)}) async-start(bf16[128,16,128]{2,1,0:T(8,128)(2,1)} %get-tuple-element.35), calls=%async_computation.2 | async-start | bytes 1048576 | tf_op jit(solution)/shard_map/all_to_all | solution.py:574
  148.6 13.4 %copy-start.1 = (bf16[2048,512]{1,0:T(8,128)(2,1)S(1)}, bf16[2048,512]{1,0:T(8,128)(2,1)}, u32[]{:S(2)}) copy-start(bf16[2048,512]{1,0:T(8,128)(2,1)} %x_own.1) | copy-start | bytes 6291460
  148.6 30.0 %all-to-all-start.4 = ((f32[128,16,128]{2,1,0:T(8,128)}), f32[128,16,128]{2,1,0:T(8,128)}, u32[]{:S(2)}, u32[]{:S(2)}) async-start(f32[128,16,128]{2,1,0:T(8,128)} %get-tuple-element.42), calls=%async_computation.4 | async-start | bytes 2097152 | tf_op jit(solution)/shard_map/all_to_all | solution.py:585
  154.5 7.5 %copy-start.2 = (bf16[2048,128]{1,0:T(8,128)(2,1)S(1)}, bf16[2048,128]{1,0:T(8,128)(2,1)}, u32[]{:S(2)}) copy-start(bf16[2048,128]{1,0:T(8,128)(2,1)} %w_out_ref.3) | copy-start | bytes 1572868
  159.8 2.3 collective-permute-start.1
  178.6 47.1 %all-to-all-start.5 = ((f32[64,80,128]{2,1,0:T(8,128)}), f32[64,80,128]{2,1,0:T(8,128)}, u32[]{:S(2)}, u32[]{:S(2)}) async-start(f32[64,80,128]{2,1,0:T(8,128)} %land_backward.1), calls=%async_computation.5 | async-start | bytes 5242880 | tf_op jit(solution)/shard_map/all_to_all | solution.py:599
  227.6 1.3 collective-permute-start.2

commit v4 on v3

--- a/solution.py
+++ b/solution.py
@@ -11,7 +11,7 @@
 
 STEPS = 4
 REACH = 4
-CHUNK = 64
+CHUNK = 128
 TY = ("y", "core")
 TX = ("z", "x")
 ALL = TY + TX
@@ -507,7 +507,7 @@
         out_specs=block_spec,
         compiler_params=pltpu.CompilerParams(vmem_limit_bytes=40 << 20),
         name="pick_rows",
-    )(*in_hbm(index, table), *more)
+    )(index, *in_hbm(table), *more)
 
 
 def other_core(values):

time: 232 us -> 231 us (level)
    unnamed x31 -> x29, local copies, waits for them, and re-layouts: 6.45 us -> 6.9 us
  transfers between devices with their start and end apart: 8 -> 8, of which waited for: 6 -> 6; matrix products, arithmetic and copies ran while one was open for 7% -> 6% of each run, Pallas kernels for 20% -> 20%
where the time goes in v4:
time: 231 us; the launch traced here: 229 us
  Pallas kernels  82 us (35%)
  waiting for transfers between devices  62.3 us (27%)
  starting transfers between devices  40.2 us (17%)
  blocking collectives  23.7 us (10%)
  local copies, waits for them, and re-layouts  13.8 us (6%)
  other arithmetic  5.87 us (3%)
    all_to_all x1, waiting for transfers between devices, local(): pieces = lax.all_to_all(pieces, ('y', 'z', 'x'), 0, 0)  33.9 us
    all_to_all x1, blocking collectives, local(): lax.all_to_all(back_values.reshape(devices, slot_count, species), ALL, sp...  23.7 us
    pallas_call x1, Pallas kernels, backward(): pl.pallas_call(backward_body, out_shape=jax.ShapeDtypeStruct((peers, send...  16.6 us
    pallas_call x2, Pallas kernels, gates(): pl.pallas_call(gates_body, out_shape=[pltpu.HBM((rows, hid // 2), BF16),...  16.5 us
    pallas_call x1, Pallas kernels, raster(): pl.pallas_call(functools.partial(raster_body, scale), out_shape=[pltpu.HB...  15.4 us
    all_to_all x1, starting transfers between devices, local(): got = lax.all_to_all(send, ALL, split_axis=0, concat_axis=0, tiled=True)  11.6 us
    pallas_call x2, Pallas kernels, pick(): pl.pallas_call(functools.partial(pick_body, wide), out_shape=jax.ShapeDty...  10.8 us
    pallas_call x1, Pallas kernels, forward(): pl.pallas_call(forward_body, out_shape=jax.ShapeDtypeStruct((rows, specie...  10.8 us
  transfers between devices with their start and end apart: 8, of which 6 were waited for; matrix products, arithmetic and copies ran while one was open for 6% of the time, Pallas kernels for 20%

profile of v4, /device:TPU:0, one launch (start us, length us, event | category | flops | bytes accessed | tf_op | source)
XLA Modules:
  0.0 228.7 jit_solution(1863221396588135263)
XLA Ops:
  2.0 10.8 %land_forward.1.intensity_ref.refs_0_ = f32[2048,128]{1,0:T(8,128)S(1)} custom-call(bf16[2048,512]{1,0:T(8,128)(2,1)} %x_own.1, bf16[512,2048]{1,0:T(8,128)(2,1)} %w_in_ref.5, f32[1,2048]{1,0:T(1,128)S(1)} %bitcast.46, bf16[2048,128]{1,0:T(8,128)(2,1)} %w_out_ref.3, f32[1,128]{1,0:T(1,128)S(1)} %bitcast.51), custom_call_target="tpu_custom_call" | custom-call | tf_op jit(solution)/shard_map/land_forward/pallas_call | solution.py:186
  12.8 4.2 %pack_cells.1 = (bf16[128,40,128]{2,1,0:T(8,128)(2,1)}, s32[1,2048]{1,0:T(1,128)S(1)}) custom-call(s32[1,2048]{1,0:T(1,128)S(1)} %bitcast.49, s32[1,2048]{1,0:T(1,128)S(1)} %bitcast.50, f32[2048,128]{1,0:T(8,128)S(1)} %land_forward.1.intensity_ref.refs_0_), custom_call_target="tpu_custom_call" | custom-call | tf_op jit(solution)/shard_map/pack_cells/pallas_call | solution.py:389
  17.0 11.6 %all-to-all-start = ((bf16[128,40,128]{2,1,0:T(8,128)(2,1)}), bf16[128,40,128]{2,1,0:T(8,128)(2,1)}, u32[]{:S(2)}, u32[]{:S(2)}) async-start(bf16[128,40,128]{2,1,0:T(8,128)(2,1)} %get-tuple-element.25), calls=%async_computation | async-start | bytes 2621440 | tf_op jit(solution)/shard_map/all_to_all | solution.py:552
  28.9 2.4 %select_convert_fusion = bf16[16,128,128]{2,1,0:T(8,128)(2,1)} fusion(s32[16,128,128]{2,1,0:T(8,128)} %param.24, pred[16,128]{1,0:T(8,128)(4,1)S(1)} %broadcast_compare_fusion), kind=kLoop, calls=%fused_computation.1 | loop fusion | flops 524288 | bytes 1574912 | tf_op jit(solution)/shard_map/convert_element_type | solution.py:560
  31.3 2.0 copy.48
  33.3 2.0 copy.57
  35.3 8.3 %land_gates.2 = (bf16[2048,1024]{1,0:T(8,128)(2,1)}, f32[2048,1024]{1,0:T(8,128)}) custom-call(s32[1]{0:T(128)} %bitcast.core_ref, bf16[2048,512]{1,0:T(8,128)(2,1)} %x_own.1, bf16[512,2048]{1,0:T(8,128)(2,1)} %w_in_ref.5, f32[1,2048]{1,0:T(1,128)S(1)} %bitcast.47), custom_call_target="tpu_custom_call" | custom-call | tf_op jit(solution)/shard_map/land_gates/pallas_call | solution.py:217
  43.6 6.4 %all-to-all-done.got_ref = bf16[128,40,128]{2,1,0:T(8,128)(2,1)} async-done(((bf16[128,40,128]{2,1,0:T(8,128)(2,1)}), bf16[128,40,128]{2,1,0:T(8,128)(2,1)}, u32[]{:S(2)}, u32[]{:S(2)}) %all-to-all-start) | async-done | bytes 1310752 | tf_op jit(solution)/shard_map/all_to_all | solution.py:552
  50.0 7.7 %place_cells.1 = bf16[128,32,128]{2,1,0:T(8,128)(2,1)} custom-call(bf16[128,40,128]{2,1,0:T(8,128)(2,1)} %all-to-all-done.got_ref, bf16[128,16,128]{2,1,0:T(8,128)(2,1)} %bitcast.57), custom_call_target="tpu_custom_call" | custom-call | tf_op jit(solution)/shard_map/place_cells/pallas_call | solution.py:454
  57.8 6.0 %all-to-all-start.1 = ((bf16[128,32,128]{2,1,0:T(8,128)(2,1)}), bf16[128,32,128]{2,1,0:T(8,128)(2,1)}, u32[]{:S(2)}, u32[]{:S(2)}) async-start(bf16[128,32,128]{2,1,0:T(8,128)(2,1)} %place_cells.1), calls=%async_computation.1 | async-start | bytes 2097152 | tf_op jit(solution)/shard_map/all_to_all | solution.py:569
  64.0 8.2 %land_gates.3 = (bf16[2048,1024]{1,0:T(8,128)(2,1)}, f32[2048,1024]{1,0:T(8,128)}) custom-call(s32[1]{0:T(128)} %bitcast.core_ref, bf16[2048,512]{1,0:T(8,128)(2,1)} %collective-permute-done.x_ref.x_other, bf16[512,2048]{1,0:T(8,128)(2,1)} %w_in_ref.5, f32[1,2048]{1,0:T(1,128)S(1)} %bitcast.48), custom_call_target="tpu_custom_call" | custom-call | tf_op jit(solution)/shard_map/land_gates/pallas_call | solution.py:217
  72.2 9.9 %all-to-all-done.1.got_ref = bf16[128,32,128]{2,1,0:T(8,128)(2,1)} async-done(((bf16[128,32,128]{2,1,0:T(8,128)(2,1)}), bf16[128,32,128]{2,1,0:T(8,128)(2,1)}, u32[]{:S(2)}, u32[]{:S(2)}) %all-to-all-start.1) | async-done | bytes 1048608 | tf_op jit(solution)/shard_map/all_to_all | solution.py:569
  82.1 15.4 %raster_steps.1 = (f32[128,16,128]{2,1,0:T(8,128)}, bf16[128,16,128]{2,1,0:T(8,128)(2,1)}) custom-call(f32[1,32]{1,0:T(1,128)S(1)} %pad_dynamic-slice_fusion.species_ref, bf16[128,32,128]{2,1,0:T(8,128)(2,1)} %all-to-all-done.1.got_ref), custom_call_target="tpu_custom_call" | custom-call | tf_op jit(solution)/shard_map/raster_steps/pallas_call | solution.py:147
  97.6 5.7 %all-to-all-start.2 = ((bf16[128,16,128]{2,1,0:T(8,128)(2,1)}), bf16[128,16,128]{2,1,0:T(8,128)(2,1)}, u32[]{:S(2)}, u32[]{:S(2)}) async-start(bf16[128,16,128]{2,1,0:T(8,128)(2,1)} %get-tuple-element.35), calls=%async_computation.2 | async-start | bytes 1048576 | tf_op jit(solution)/shard_map/all_to_all | solution.py:574
  104.8 2.1 reshape.100.index_ref
  107.0 9.5 %all-to-all-done.2 = bf16[128,16,128]{2,1,0:T(8,128)(2,1)} async-done(((bf16[128,16,128]{2,1,0:T(8,128)(2,1)}), bf16[128,16,128]{2,1,0:T(8,128)(2,1)}, u32[]{:S(2)}, u32[]{:S(2)}) %all-to-all-start.2) | async-done | bytes 524320 | tf_op jit(solution)/shard_map/all_to_all | solution.py:574
  116.5 2.0 copy.63
  118.5 5.6 %pick_rows.2 = bf16[4096,128]{1,0:T(8,128)(2,1)S(1)} custom-call(s32[4096,1]{1,0:T(8,128)S(1)} %reshape.100.index_ref, bf16[128,2048]{1,0:T(8,128)(2,1)} %bitcast.54), custom_call_target="tpu_custom_call" | custom-call | tf_op jit(solution)/shard_map/pick_rows/pallas_call | solution.py:496
  124.1 23.7 %all_to_all.30 = bf16[128,32,128]{2,1,0:T(8,128)(2,1)} all-to-all(bf16[128,32,128]{2,1,0:T(8,128)(2,1)S(1)} %bitcast.45), channel_id=1, replica_groups=mesh['y'=4,'core'=2,'z'=4,'x'=4] {'y','core','z','x'}, dimensions={0} | all-to-all | bytes 2097152 | tf_op jit(solution)/shard_map/all_to_all | solution.py:577
  147.8 5.9 %all-to-all-start.4 = ((f32[128,16,128]{2,1,0:T(8,128)}), f32[128,16,128]{2,1,0:T(8,128)}, u32[]{:S(2)}, u32[]{:S(2)}) async-start(f32[128,16,128]{2,1,0:T(8,128)} %get-tuple-element.42), calls=%async_computation.4 | async-start | bytes 2097152 | tf_op jit(solution)/shard_map/all_to_all | solution.py:585
  153.7 5.2 %pick_rows.3.dlog_own = bf16[2048,128]{1,0:T(8,128)(2,1)S(1)} custom-call(s32[1,2048]{1,0:T(1,128)S(1)} %get-tuple-element.31.index_ref, bf16[4096,128]{1,0:T(8,128)(2,1)} %bitcast.52, f32[2048,128]{1,0:T(8,128)S(1)} %land_forward.1.intensity_ref.refs_0_), custom_call_target="tpu_custom_call" | custom-call | tf_op jit(solution)/shard_map/pick_rows/pallas_call | solution.py:496
  161.2 16.6 %land_backward.1 = f32[64,80,128]{2,1,0:T(8,128)} custom-call(s32[1]{0:T(128)} %bitcast.core_ref, bf16[2048,512]{1,0:T(8,128)(2,1)S(1)} %copy-done.1, bf16[2048,512]{1,0:T(8,128)(2,1)} %collective-permute-done.x_ref.x_other, bf16[2048,128]{1,0:T(8,128)(2,1)S(1)} %pick_rows.3.dlog_own, bf16[2048,128]{1,0:T(8,128)(2,1)S(1)} %collective-permute-done.1.dlog_other, ...), custom_call_target="tpu_custom_call" | custom-call | tf_op jit(solution)/shard_map/land_backward/pallas_call | solution.py:314
  177.7 10.3 %all-to-all-start.5 = ((f32[64,80,128]{2,1,0:T(8,128)}), f32[64,80,128]{2,1,0:T(8,128)}, u32[]{:S(2)}, u32[]{:S(2)}) async-start(f32[64,80,128]{2,1,0:T(8,128)} %land_backward.1), calls=%async_computation.5 | async-start | bytes 5242880 | tf_op jit(solution)/shard_map/all_to_all | solution.py:599
  190.9 33.9 %all-to-all-done.5 = f32[64,80,128]{2,1,0:T(8,128)} async-done(((f32[64,80,128]{2,1,0:T(8,128)}), f32[64,80,128]{2,1,0:T(8,128)}, u32[]{:S(2)}, u32[]{:S(2)}) %all-to-all-start.5) | async-done | bytes 2621472 | tf_op jit(solution)/shard_map/all_to_all | solution.py:599
  (51 shorter events, 12.3 us)
Async XLA Ops:
  0.6 0.7 copy-start.3
  1.3 0.7 copy-start.7
  2.0 10.8 %copy-start.5 = (s32[2048,1]{0,1:T(1,128)S(1)}, s32[2048,1]{0,1:T(1,128)}, u32[]{:S(2)}) copy-start(s32[2048,1]{0,1:T(1,128)} %param.18) | copy-start | bytes 24580
  2.0 10.8 %copy-start.6 = (s32[2048]{0:T(1024)S(1)}, s32[2048]{0:T(1024)}, u32[]{:S(2)}) copy-start(s32[2048]{0:T(1024)} %param.19) | copy-start | bytes 24580
  12.8 15.8 %copy-start = (bf16[2048,512]{1,0:T(8,128)(2,1)S(1)}, bf16[2048,512]{1,0:T(8,128)(2,1)}, u32[]{:S(2)}) copy-start(bf16[2048,512]{1,0:T(8,128)(2,1)} %x_own.1) | copy-start | bytes 6291460
  12.8 16.1 %copy-start.10 = (s32[16,128]{1,0:T(8,128)S(1)}, s32[16,128]{1,0:T(8,128)}, u32[]{:S(2)}) copy-start(s32[16,128]{1,0:T(8,128)} %param.25) | copy-start | bytes 24580
  17.0 33.0 %all-to-all-start = ((bf16[128,40,128]{2,1,0:T(8,128)(2,1)}), bf16[128,40,128]{2,1,0:T(8,128)(2,1)}, u32[]{:S(2)}, u32[]{:S(2)}) async-start(bf16[128,40,128]{2,1,0:T(8,128)(2,1)} %get-tuple-element.25), calls=%async_computation | async-start | bytes 2621440 | tf_op jit(solution)/shard_map/all_to_all | solution.py:552
  28.6 6.7 %copy-start.4 = (f32[2048]{0:T(1024)S(1)}, f32[2048]{0:T(1024)}, u32[]{:S(2)}) copy-start(f32[2048]{0:T(1024)} %param.15) | copy-start | bytes 24580
  28.6 35.4 %collective-permute-start = (bf16[2048,512]{1,0:T(8,128)(2,1)S(1)}, bf16[2048,512]{1,0:T(8,128)(2,1)}, u32[]{:S(2)}, u32[]{:S(2)}) collective-permute-start(bf16[2048,512]{1,0:T(8,128)(2,1)S(1)} %copy-done), channel_id=1, source_target_pairs={{0,16},{16,0},{1,17},{17,1},{2,18},{18,2},{3,19},{19,3},{4,20},{20... | collective-permute-start | bytes 6291464 | tf_op jit(solution)/shard_map/ppermute | solution.py:514
  50.0 13.7 %copy-start.9 = (f32[128,9]{0,1:T(8,128)S(1)}, f32[128,9]{0,1:T(8,128)}, u32[]{:S(2)}) copy-start(f32[128,9]{0,1:T(8,128)} %param.20) | copy-start | bytes 13828
  50.0 13.8 %copy-start.8 = (f32[128,9]{0,1:T(8,128)S(1)}, f32[128,9]{0,1:T(8,128)}, u32[]{:S(2)}) copy-start(f32[128,9]{0,1:T(8,128)} %param.21) | copy-start | bytes 13828
  50.0 13.8 %copy-start.11 = (f32[128]{0:T(128)S(1)}, f32[128]{0:T(128)}, u32[]{:S(2)}) copy-start(f32[128]{0:T(128)} %param.23) | copy-start | bytes 1540
  50.0 13.8 %copy-start.12 = (f32[128]{0:T(128)S(1)}, f32[128]{0:T(128)}, u32[]{:S(2)}) copy-start(f32[128]{0:T(128)} %param.22) | copy-start | bytes 1540
  57.8 24.4 %all-to-all-start.1 = ((bf16[128,32,128]{2,1,0:T(8,128)(2,1)}), bf16[128,32,128]{2,1,0:T(8,128)(2,1)}, u32[]{:S(2)}, u32[]{:S(2)}) async-start(bf16[128,32,128]{2,1,0:T(8,128)(2,1)} %place_cells.1), calls=%async_computation.1 | async-start | bytes 2097152 | tf_op jit(solution)/shard_map/all_to_all | solution.py:569
  97.6 18.9 %all-to-all-start.2 = ((bf16[128,16,128]{2,1,0:T(8,128)(2,1)}), bf16[128,16,128]{2,1,0:T(8,128)(2,1)}, u32[]{:S(2)}, u32[]{:S(2)}) async-start(bf16[128,16,128]{2,1,0:T(8,128)(2,1)} %get-tuple-element.35), calls=%async_computation.2 | async-start | bytes 1048576 | tf_op jit(solution)/shard_map/all_to_all | solution.py:574
  147.8 13.4 %copy-start.1 = (bf16[2048,512]{1,0:T(8,128)(2,1)S(1)}, bf16[2048,512]{1,0:T(8,128)(2,1)}, u32[]{:S(2)}) copy-start(bf16[2048,512]{1,0:T(8,128)(2,1)} %x_own.1) | copy-start | bytes 6291460
  147.8 30.0 %all-to-all-start.4 = ((f32[128,16,128]{2,1,0:T(8,128)}), f32[128,16,128]{2,1,0:T(8,128)}, u32[]{:S(2)}, u32[]{:S(2)}) async-start(f32[128,16,128]{2,1,0:T(8,128)} %get-tuple-element.42), calls=%async_computation.4 | async-start | bytes 2097152 | tf_op jit(solution)/shard_map/all_to_all | solution.py:585
  153.7 7.5 %copy-start.2 = (bf16[2048,128]{1,0:T(8,128)(2,1)S(1)}, bf16[2048,128]{1,0:T(8,128)(2,1)}, u32[]{:S(2)}) copy-start(bf16[2048,128]{1,0:T(8,128)(2,1)} %w_out_ref.3) | copy-start | bytes 1572868
  158.9 2.3 collective-permute-start.1
  177.7 47.1 %all-to-all-start.5 = ((f32[64,80,128]{2,1,0:T(8,128)}), f32[64,80,128]{2,1,0:T(8,128)}, u32[]{:S(2)}, u32[]{:S(2)}) async-start(f32[64,80,128]{2,1,0:T(8,128)} %land_backward.1), calls=%async_computation.5 | async-start | bytes 5242880 | tf_op jit(solution)/shard_map/all_to_all | solution.py:599
  226.8 1.3 collective-permute-start.2

commit v5 on v4

--- a/solution.py
+++ b/solution.py
@@ -487,7 +487,7 @@
     out_ref[...] = picked.astype(BF16)
 
 
-def pick(index, table, factors=None, wide=False, block=512):
+def pick(index, table, factors=None, wide=False, block=1024):
     rows = index.size
     column = index.shape[1] == 1
     lanes = table.shape[0] if wide else table.shape[1]

time: 231 us -> 229 us (level)
  no operation moved by 1% of the time
where the time goes in v5:
time: 229 us; the launch traced here: 227 us
  Pallas kernels  80 us (35%)
  waiting for transfers between devices  62.3 us (27%)
  starting transfers between devices  39.9 us (17%)
  blocking collectives  23.7 us (10%)
  local copies, waits for them, and re-layouts  13.8 us (6%)
  other arithmetic  5.87 us (3%)
    all_to_all x1, waiting for transfers between devices, local(): pieces = lax.all_to_all(pieces, ('y', 'z', 'x'), 0, 0)  34 us
    all_to_all x1, blocking collectives, local(): lax.all_to_all(back_values.reshape(devices, slot_count, species), ALL, sp...  23.7 us
    pallas_call x1, Pallas kernels, backward(): pl.pallas_call(backward_body, out_shape=jax.ShapeDtypeStruct((peers, send...  16.6 us
    pallas_call x2, Pallas kernels, gates(): pl.pallas_call(gates_body, out_shape=[pltpu.HBM((rows, hid // 2), BF16),...  16.5 us
    pallas_call x1, Pallas kernels, raster(): pl.pallas_call(functools.partial(raster_body, scale), out_shape=[pltpu.HB...  15.4 us
    all_to_all x1, starting transfers between devices, local(): got = lax.all_to_all(send, ALL, split_axis=0, concat_axis=0, tiled=True)  11.6 us
    pallas_call x1, Pallas kernels, forward(): pl.pallas_call(forward_body, out_shape=jax.ShapeDtypeStruct((rows, specie...  10.8 us
    all_to_all x1, starting transfers between devices, local(): pieces = lax.all_to_all(pieces, ('y', 'z', 'x'), 0, 0)  10 us
  transfers between devices with their start and end apart: 8, of which 6 were waited for; matrix products, arithmetic and copies ran while one was open for 6% of the time, Pallas kernels for 20%

profile of v5, /device:TPU:0, one launch (start us, length us, event | category | flops | bytes accessed | tf_op | source)
XLA Modules:
  0.0 226.6 jit_solution(13617651471000256877)
XLA Ops:
  2.0 10.8 %land_forward.1.intensity_ref.refs_0_ = f32[2048,128]{1,0:T(8,128)S(1)} custom-call(bf16[2048,512]{1,0:T(8,128)(2,1)} %x_own.1, bf16[512,2048]{1,0:T(8,128)(2,1)} %w_in_ref.5, f32[1,2048]{1,0:T(1,128)S(1)} %bitcast.46, bf16[2048,128]{1,0:T(8,128)(2,1)} %w_out_ref.3, f32[1,128]{1,0:T(1,128)S(1)} %bitcast.51), custom_call_target="tpu_custom_call" | custom-call | tf_op jit(solution)/shard_map/land_forward/pallas_call | solution.py:186
  12.8 4.2 %pack_cells.1 = (bf16[128,40,128]{2,1,0:T(8,128)(2,1)}, s32[1,2048]{1,0:T(1,128)S(1)}) custom-call(s32[1,2048]{1,0:T(1,128)S(1)} %bitcast.49, s32[1,2048]{1,0:T(1,128)S(1)} %bitcast.50, f32[2048,128]{1,0:T(8,128)S(1)} %land_forward.1.intensity_ref.refs_0_), custom_call_target="tpu_custom_call" | custom-call | tf_op jit(solution)/shard_map/pack_cells/pallas_call | solution.py:389
  17.0 11.6 %all-to-all-start = ((bf16[128,40,128]{2,1,0:T(8,128)(2,1)}), bf16[128,40,128]{2,1,0:T(8,128)(2,1)}, u32[]{:S(2)}, u32[]{:S(2)}) async-start(bf16[128,40,128]{2,1,0:T(8,128)(2,1)} %get-tuple-element.25), calls=%async_computation | async-start | bytes 2621440 | tf_op jit(solution)/shard_map/all_to_all | solution.py:552
  28.9 2.4 %select_convert_fusion = bf16[16,128,128]{2,1,0:T(8,128)(2,1)} fusion(s32[16,128,128]{2,1,0:T(8,128)} %param.24, pred[16,128]{1,0:T(8,128)(4,1)S(1)} %broadcast_compare_fusion), kind=kLoop, calls=%fused_computation.1 | loop fusion | flops 524288 | bytes 1574912 | tf_op jit(solution)/shard_map/convert_element_type | solution.py:560
  31.3 2.0 copy.48
  33.3 2.0 copy.57
  35.3 8.3 %land_gates.2 = (bf16[2048,1024]{1,0:T(8,128)(2,1)}, f32[2048,1024]{1,0:T(8,128)}) custom-call(s32[1]{0:T(128)} %bitcast.core_ref, bf16[2048,512]{1,0:T(8,128)(2,1)} %x_own.1, bf16[512,2048]{1,0:T(8,128)(2,1)} %w_in_ref.5, f32[1,2048]{1,0:T(1,128)S(1)} %bitcast.47), custom_call_target="tpu_custom_call" | custom-call | tf_op jit(solution)/shard_map/land_gates/pallas_call | solution.py:217
  43.6 6.4 %all-to-all-done.got_ref = bf16[128,40,128]{2,1,0:T(8,128)(2,1)} async-done(((bf16[128,40,128]{2,1,0:T(8,128)(2,1)}), bf16[128,40,128]{2,1,0:T(8,128)(2,1)}, u32[]{:S(2)}, u32[]{:S(2)}) %all-to-all-start) | async-done | bytes 1310752 | tf_op jit(solution)/shard_map/all_to_all | solution.py:552
  50.0 7.7 %place_cells.1 = bf16[128,32,128]{2,1,0:T(8,128)(2,1)} custom-call(bf16[128,40,128]{2,1,0:T(8,128)(2,1)} %all-to-all-done.got_ref, bf16[128,16,128]{2,1,0:T(8,128)(2,1)} %bitcast.57), custom_call_target="tpu_custom_call" | custom-call | tf_op jit(solution)/shard_map/place_cells/pallas_call | solution.py:454
  57.8 6.0 %all-to-all-start.1 = ((bf16[128,32,128]{2,1,0:T(8,128)(2,1)}), bf16[128,32,128]{2,1,0:T(8,128)(2,1)}, u32[]{:S(2)}, u32[]{:S(2)}) async-start(bf16[128,32,128]{2,1,0:T(8,128)(2,1)} %place_cells.1), calls=%async_computation.1 | async-start | bytes 2097152 | tf_op jit(solution)/shard_map/all_to_all | solution.py:569
  64.0 8.2 %land_gates.3 = (bf16[2048,1024]{1,0:T(8,128)(2,1)}, f32[2048,1024]{1,0:T(8,128)}) custom-call(s32[1]{0:T(128)} %bitcast.core_ref, bf16[2048,512]{1,0:T(8,128)(2,1)} %collective-permute-done.x_ref.x_other, bf16[512,2048]{1,0:T(8,128)(2,1)} %w_in_ref.5, f32[1,2048]{1,0:T(1,128)S(1)} %bitcast.48), custom_call_target="tpu_custom_call" | custom-call | tf_op jit(solution)/shard_map/land_gates/pallas_call | solution.py:217
  72.2 9.9 %all-to-all-done.1.got_ref = bf16[128,32,128]{2,1,0:T(8,128)(2,1)} async-done(((bf16[128,32,128]{2,1,0:T(8,128)(2,1)}), bf16[128,32,128]{2,1,0:T(8,128)(2,1)}, u32[]{:S(2)}, u32[]{:S(2)}) %all-to-all-start.1) | async-done | bytes 1048608 | tf_op jit(solution)/shard_map/all_to_all | solution.py:569
  82.1 15.4 %raster_steps.1 = (f32[128,16,128]{2,1,0:T(8,128)}, bf16[128,16,128]{2,1,0:T(8,128)(2,1)}) custom-call(f32[1,32]{1,0:T(1,128)S(1)} %pad_dynamic-slice_fusion.species_ref, bf16[128,32,128]{2,1,0:T(8,128)(2,1)} %all-to-all-done.1.got_ref), custom_call_target="tpu_custom_call" | custom-call | tf_op jit(solution)/shard_map/raster_steps/pallas_call | solution.py:147
  97.6 5.7 %all-to-all-start.2 = ((bf16[128,16,128]{2,1,0:T(8,128)(2,1)}), bf16[128,16,128]{2,1,0:T(8,128)(2,1)}, u32[]{:S(2)}, u32[]{:S(2)}) async-start(bf16[128,16,128]{2,1,0:T(8,128)(2,1)} %get-tuple-element.35), calls=%async_computation.2 | async-start | bytes 1048576 | tf_op jit(solution)/shard_map/all_to_all | solution.py:574
  104.8 2.1 reshape.100.index_ref
  107.0 9.5 %all-to-all-done.2 = bf16[128,16,128]{2,1,0:T(8,128)(2,1)} async-done(((bf16[128,16,128]{2,1,0:T(8,128)(2,1)}), bf16[128,16,128]{2,1,0:T(8,128)(2,1)}, u32[]{:S(2)}, u32[]{:S(2)}) %all-to-all-start.2) | async-done | bytes 524320 | tf_op jit(solution)/shard_map/all_to_all | solution.py:574
  116.5 2.0 copy.63
  118.5 4.2 %pick_rows.2 = bf16[4096,128]{1,0:T(8,128)(2,1)S(1)} custom-call(s32[4096,1]{1,0:T(8,128)S(1)} %reshape.100.index_ref, bf16[128,2048]{1,0:T(8,128)(2,1)} %bitcast.54), custom_call_target="tpu_custom_call" | custom-call | tf_op jit(solution)/shard_map/pick_rows/pallas_call | solution.py:496
  122.7 23.7 %all_to_all.30 = bf16[128,32,128]{2,1,0:T(8,128)(2,1)} all-to-all(bf16[128,32,128]{2,1,0:T(8,128)(2,1)S(1)} %bitcast.45), channel_id=1, replica_groups=mesh['y'=4,'core'=2,'z'=4,'x'=4] {'y','core','z','x'}, dimensions={0} | all-to-all | bytes 2097152 | tf_op jit(solution)/shard_map/all_to_all | solution.py:577
  146.4 6.2 %all-to-all-start.4 = ((f32[128,16,128]{2,1,0:T(8,128)}), f32[128,16,128]{2,1,0:T(8,128)}, u32[]{:S(2)}, u32[]{:S(2)}) async-start(f32[128,16,128]{2,1,0:T(8,128)} %get-tuple-element.42), calls=%async_computation.4 | async-start | bytes 2097152 | tf_op jit(solution)/shard_map/all_to_all | solution.py:585
  152.6 4.7 %pick_rows.3.dlog_own = bf16[2048,128]{1,0:T(8,128)(2,1)S(1)} custom-call(s32[1,2048]{1,0:T(1,128)S(1)} %get-tuple-element.31.index_ref, bf16[4096,128]{1,0:T(8,128)(2,1)} %bitcast.52, f32[2048,128]{1,0:T(8,128)S(1)} %land_forward.1.intensity_ref.refs_0_), custom_call_target="tpu_custom_call" | custom-call | tf_op jit(solution)/shard_map/pick_rows/pallas_call | solution.py:496
  159.2 16.6 %land_backward.1 = f32[64,80,128]{2,1,0:T(8,128)} custom-call(s32[1]{0:T(128)} %bitcast.core_ref, bf16[2048,512]{1,0:T(8,128)(2,1)S(1)} %copy-done.1, bf16[2048,512]{1,0:T(8,128)(2,1)} %collective-permute-done.x_ref.x_other, bf16[2048,128]{1,0:T(8,128)(2,1)S(1)} %pick_rows.3.dlog_own, bf16[2048,128]{1,0:T(8,128)(2,1)S(1)} %collective-permute-done.1.dlog_other, ...), custom_call_target="tpu_custom_call" | custom-call | tf_op jit(solution)/shard_map/land_backward/pallas_call | solution.py:314
  175.8 10.0 %all-to-all-start.5 = ((f32[64,80,128]{2,1,0:T(8,128)}), f32[64,80,128]{2,1,0:T(8,128)}, u32[]{:S(2)}, u32[]{:S(2)}) async-start(f32[64,80,128]{2,1,0:T(8,128)} %land_backward.1), calls=%async_computation.5 | async-start | bytes 5242880 | tf_op jit(solution)/shard_map/all_to_all | solution.py:599
  188.7 34.0 %all-to-all-done.5 = f32[64,80,128]{2,1,0:T(8,128)} async-done(((f32[64,80,128]{2,1,0:T(8,128)}), f32[64,80,128]{2,1,0:T(8,128)}, u32[]{:S(2)}, u32[]{:S(2)}) %all-to-all-start.5) | async-done | bytes 2621472 | tf_op jit(solution)/shard_map/all_to_all | solution.py:599
  (51 shorter events, 12.1 us)
Async XLA Ops:
  0.6 0.7 copy-start.3
  1.3 0.7 copy-start.7
  2.0 10.8 %copy-start.5 = (s32[2048,1]{0,1:T(1,128)S(1)}, s32[2048,1]{0,1:T(1,128)}, u32[]{:S(2)}) copy-start(s32[2048,1]{0,1:T(1,128)} %param.18) | copy-start | bytes 24580
  2.0 10.8 %copy-start.6 = (s32[2048]{0:T(1024)S(1)}, s32[2048]{0:T(1024)}, u32[]{:S(2)}) copy-start(s32[2048]{0:T(1024)} %param.19) | copy-start | bytes 24580
  12.8 15.8 %copy-start = (bf16[2048,512]{1,0:T(8,128)(2,1)S(1)}, bf16[2048,512]{1,0:T(8,128)(2,1)}, u32[]{:S(2)}) copy-start(bf16[2048,512]{1,0:T(8,128)(2,1)} %x_own.1) | copy-start | bytes 6291460
  12.8 16.1 %copy-start.10 = (s32[16,128]{1,0:T(8,128)S(1)}, s32[16,128]{1,0:T(8,128)}, u32[]{:S(2)}) copy-start(s32[16,128]{1,0:T(8,128)} %param.25) | copy-start | bytes 24580
  17.0 33.0 %all-to-all-start = ((bf16[128,40,128]{2,1,0:T(8,128)(2,1)}), bf16[128,40,128]{2,1,0:T(8,128)(2,1)}, u32[]{:S(2)}, u32[]{:S(2)}) async-start(bf16[128,40,128]{2,1,0:T(8,128)(2,1)} %get-tuple-element.25), calls=%async_computation | async-start | bytes 2621440 | tf_op jit(solution)/shard_map/all_to_all | solution.py:552
  28.6 6.7 %copy-start.4 = (f32[2048]{0:T(1024)S(1)}, f32[2048]{0:T(1024)}, u32[]{:S(2)}) copy-start(f32[2048]{0:T(1024)} %param.15) | copy-start | bytes 24580
  28.6 35.4 %collective-permute-start = (bf16[2048,512]{1,0:T(8,128)(2,1)S(1)}, bf16[2048,512]{1,0:T(8,128)(2,1)}, u32[]{:S(2)}, u32[]{:S(2)}) collective-permute-start(bf16[2048,512]{1,0:T(8,128)(2,1)S(1)} %copy-done), channel_id=1, source_target_pairs={{0,16},{16,0},{1,17},{17,1},{2,18},{18,2},{3,19},{19,3},{4,20},{20... | collective-permute-start | bytes 6291464 | tf_op jit(solution)/shard_map/ppermute | solution.py:514
  50.0 13.7 %copy-start.9 = (f32[128,9]{0,1:T(8,128)S(1)}, f32[128,9]{0,1:T(8,128)}, u32[]{:S(2)}) copy-start(f32[128,9]{0,1:T(8,128)} %param.20) | copy-start | bytes 13828
  50.0 13.8 %copy-start.8 = (f32[128,9]{0,1:T(8,128)S(1)}, f32[128,9]{0,1:T(8,128)}, u32[]{:S(2)}) copy-start(f32[128,9]{0,1:T(8,128)} %param.21) | copy-start | bytes 13828
  50.0 13.8 %copy-start.11 = (f32[128]{0:T(128)S(1)}, f32[128]{0:T(128)}, u32[]{:S(2)}) copy-start(f32[128]{0:T(128)} %param.23) | copy-start | bytes 1540
  50.0 13.8 %copy-start.12 = (f32[128]{0:T(128)S(1)}, f32[128]{0:T(128)}, u32[]{:S(2)}) copy-start(f32[128]{0:T(128)} %param.22) | copy-start | bytes 1540
  57.8 24.4 %all-to-all-start.1 = ((bf16[128,32,128]{2,1,0:T(8,128)(2,1)}), bf16[128,32,128]{2,1,0:T(8,128)(2,1)}, u32[]{:S(2)}, u32[]{:S(2)}) async-start(bf16[128,32,128]{2,1,0:T(8,128)(2,1)} %place_cells.1), calls=%async_computation.1 | async-start | bytes 2097152 | tf_op jit(solution)/shard_map/all_to_all | solution.py:569
  97.6 18.9 %all-to-all-start.2 = ((bf16[128,16,128]{2,1,0:T(8,128)(2,1)}), bf16[128,16,128]{2,1,0:T(8,128)(2,1)}, u32[]{:S(2)}, u32[]{:S(2)}) async-start(bf16[128,16,128]{2,1,0:T(8,128)(2,1)} %get-tuple-element.35), calls=%async_computation.2 | async-start | bytes 1048576 | tf_op jit(solution)/shard_map/all_to_all | solution.py:574
  146.4 12.8 %copy-start.1 = (bf16[2048,512]{1,0:T(8,128)(2,1)S(1)}, bf16[2048,512]{1,0:T(8,128)(2,1)}, u32[]{:S(2)}) copy-start(bf16[2048,512]{1,0:T(8,128)(2,1)} %x_own.1) | copy-start | bytes 6291460
  146.4 29.4 %all-to-all-start.4 = ((f32[128,16,128]{2,1,0:T(8,128)}), f32[128,16,128]{2,1,0:T(8,128)}, u32[]{:S(2)}, u32[]{:S(2)}) async-start(f32[128,16,128]{2,1,0:T(8,128)} %get-tuple-element.42), calls=%async_computation.4 | async-start | bytes 2097152 | tf_op jit(solution)/shard_map/all_to_all | solution.py:585
  152.5 6.7 %copy-start.2 = (bf16[2048,128]{1,0:T(8,128)(2,1)S(1)}, bf16[2048,128]{1,0:T(8,128)(2,1)}, u32[]{:S(2)}) copy-start(bf16[2048,128]{1,0:T(8,128)(2,1)} %w_out_ref.3) | copy-start | bytes 1572868
  157.2 2.0 collective-permute-start.1
  175.8 46.9 %all-to-all-start.5 = ((f32[64,80,128]{2,1,0:T(8,128)}), f32[64,80,128]{2,1,0:T(8,128)}, u32[]{:S(2)}, u32[]{:S(2)}) async-start(f32[64,80,128]{2,1,0:T(8,128)} %land_backward.1), calls=%async_computation.5 | async-start | bytes 5242880 | tf_op jit(solution)/shard_map/all_to_all | solution.py:599
  224.6 1.3 collective-permute-start.2
